TPU v7x, 128 devices: a whole 4x4x4 slice. The times are simulated.
128 devices in a mesh: dp: 4 (over x_lo, core), seq: 32 (over y, x_hi, z).
Axes of the slice: x: 4 (x_hi: 2, x_lo: 2; x = x_hi * 2 + x_lo), y: 4, z: 4, core: 2. Of those that a mesh axis runs over, the one named last changes fastest.
Arguments:
- embeddings: bfloat16 [4, 32, 512, 8192], P('dp', 'seq'), may hold values from -6 to 6
- layout: int32 [4, 32, 32], P('dp'), may hold values from 0 to 31, as said below
- lengths: int32 [4], P('dp'), may hold values from 4096 to 16384, as said below
- targets: int32 [4, 4096, 2048], P('dp', 'seq'), may hold values from 0 to 7
- projection: bfloat16 [8192, 768], P('dp'), may hold values from -0.0625 to 0.0625
- kernels: bfloat16 [2, 3, 768, 384], replicated, may hold values from -0.125 to 0.125
- mixers: bfloat16 [2, 384, 768], replicated, may hold values from -0.3125 to 0.3125
- readout: bfloat16 [768, 2048], replicated, may hold values from -0.21875 to 0.21875
Outputs:
- kernel_grads: float32 [2, 3, 768, 384], P(None, None, 'seq', 'dp')
- mixer_grads: float32 [2, 384, 768], P(None, 'seq', 'dp')
- readout_grad: float32 [768, 2048], P('seq', 'dp')
- trunk_grad: float32 [4, 8192, 768], P('dp', 'seq')
Inputs may be any that keep to these rules, and one draw needn't show every extreme that they name: For every window w and shard j, layout[w, s, j] over all shards s lists every block number once. `lengths`: multiples of 128; in every draw one window has the full 16384 and another the least.
All inputs are finite; a program needn't handle non-finite values.
Results may differ from a plain program's by a relative error of at most 0.017.
Values may be sent and summed in bfloat16 or wider, within the bound.
A program may use at most 128 MiB of HBM per device.

v0:
```python
import math

import jax
import jax.numpy as jnp
from jax import lax
from jax.sharding import PartitionSpec as P

SPREAD_FINE = 256
SPREAD_COARSE = 128


def with_halo(shard, sides, width):
    for axis, dim in sides:
        size, length = (lax.axis_size(axis), shard.shape[dim])
        up = [(i, (i + 1) % size) for i in range(size - 1)]
        down = [(j, i) for i, j in up]
        last = lax.slice_in_dim(shard, length - width, length, axis=dim)
        leading = lax.slice_in_dim(shard, 0, width, axis=dim)
        before = lax.ppermute(last, axis, up)
        after = lax.ppermute(leading, axis, down)
        shard = jnp.concatenate([before, shard, after], axis=dim)
    return shard


def gelu_exact(values):
    return 0.5 * values * (1.0 + lax.erf(values * (1.0 / math.sqrt(2.0))))


def gelu_slope(values):
    cumulative = 0.5 * (1.0 + lax.erf(values * (1.0 / math.sqrt(2.0))))
    density = jnp.exp(-0.5 * values * values) * (1.0 / math.sqrt(2.0 * math.pi))
    return cumulative + values * density


def matmul(left_side, right_side):
    return jnp.dot(left_side, right_side, preferred_element_type=jnp.float32)


def times_transposed(left_side, right_side):
    return lax.dot_general(
        left_side, right_side, (((1,), (1,)), ((), ())), preferred_element_type=jnp.float32
    )


def transposed_times(left_side, right_side):
    return lax.dot_general(
        left_side, right_side, (((0,), (0,)), ((), ())), preferred_element_type=jnp.float32
    )


def spread_taps(extended, spread, row_count):
    return (
        extended[0:row_count],
        extended[spread : spread + row_count],
        extended[2 * spread : 2 * spread + row_count],
    )


def block_rest(hidden, shifted, kernel, mixing):
    inner_sum = (
        matmul(shifted[0], kernel[0])
        + matmul(shifted[1], kernel[1])
        + matmul(shifted[2], kernel[2])
    )
    gated_out = gelu_exact(inner_sum).astype(jnp.bfloat16)
    output = hidden.astype(jnp.float32) + matmul(gated_out, mixing)
    pooled = (output.reshape(-1, 2, output.shape[1]).sum(axis=1) * 0.5).astype(jnp.bfloat16)
    return (pooled, inner_sum, gated_out)


def block_backward(upstream, shifted, inner_sum, gated_out, mixing):
    mixing_grad = transposed_times(gated_out, upstream)
    inner_grad = (times_transposed(upstream, mixing) * gelu_slope(inner_sum)).astype(jnp.bfloat16)
    kernel_grad = jnp.stack(
        [transposed_times(shifted[tap_index], inner_grad) for tap_index in range(3)]
    )
    return (kernel_grad, mixing_grad, inner_grad)


def shards(embeddings, layout, lengths, targets, projection, kernels, mixers, readout):
    groups = lax.axis_size("seq")
    windows_total = lax.axis_size("dp")
    device = lax.axis_index("seq")
    local_rows = embeddings[0, 0]
    row_count = local_rows.shape[0]
    block_rows = row_count // groups
    channels = projection.shape[1]
    layout_table = layout[0]
    length = lengths[0]
    shard_ids = jnp.arange(groups, dtype=jnp.int32)
    own_column = lax.dynamic_index_in_dim(layout_table, device, axis=1, keepdims=False)
    matches = (own_column[:, None] == shard_ids[None, :]).astype(jnp.int32)
    source_index = jnp.sum(shard_ids[:, None] * matches, axis=0)
    row_ids = jnp.arange(row_count, dtype=jnp.int32)
    owner_shard = row_ids // block_rows
    own_slots = lax.dynamic_index_in_dim(layout_table, device, axis=0, keepdims=False)
    source_position = (
        owner_shard * row_count
        + jnp.take(own_slots, owner_shard) * block_rows
        + row_ids % block_rows
    )
    inside = (source_position < length).astype(jnp.float32)
    outgoing = (
        jnp.dot(
            local_rows,
            lax.all_gather(projection, "dp", axis=0, tiled=True),
            preferred_element_type=jnp.float32,
        )
        * inside[:, None]
    ).astype(jnp.bfloat16)
    received = lax.all_to_all(
        outgoing.reshape(groups, block_rows, channels),
        "seq",
        split_axis=0,
        concat_axis=0,
        tiled=True,
    )
    hidden = jnp.take(received, source_index, axis=0).reshape(row_count, channels)
    fine_spread = SPREAD_FINE
    coarse_spread = SPREAD_COARSE
    half_count = row_count // 2
    fine_active = gelu_exact(hidden.astype(jnp.float32)).astype(jnp.bfloat16)
    fine_wide = with_halo(fine_active, (("seq", 0),), fine_spread)
    fine_shifted = spread_taps(fine_wide, fine_spread, row_count)
    first_pooled, fine_inner, fine_gated = block_rest(hidden, fine_shifted, kernels[0], mixers[0])
    coarse_active = gelu_exact(first_pooled.astype(jnp.float32)).astype(jnp.bfloat16)
    coarse_wide = with_halo(coarse_active, (("seq", 0),), coarse_spread)
    coarse_shifted = spread_taps(coarse_wide, coarse_spread, half_count)
    second, coarse_inner, coarse_gated = block_rest(
        first_pooled, coarse_shifted, kernels[1], mixers[1]
    )
    bin_count = row_count // 4
    logits = matmul(second, readout)
    bin_ids = device * bin_count + jnp.arange(bin_count, dtype=jnp.int32)
    valid_bins = (bin_ids * 4 < length).astype(jnp.float32)
    loss_scale = 2.0 / math.sqrt(windows_total * groups * bin_count)
    target_values = targets[0].astype(jnp.float32)
    logit_grad = (
        loss_scale
        * valid_bins[:, None]
        * (jax.nn.softplus(logits) - target_values)
        * jax.nn.sigmoid(logits)
    ).astype(jnp.bfloat16)
    readout_grad = transposed_times(second, logit_grad)
    upper_grad = (times_transposed(logit_grad, readout) * 0.5).astype(jnp.bfloat16)
    upper_rows = jnp.repeat(upper_grad, 2, axis=0)
    coarse_kernel, coarse_mixing, coarse_grad = block_backward(
        upper_rows, coarse_shifted, coarse_inner, coarse_gated, mixers[1]
    )
    grad_wide = with_halo(coarse_grad, (("seq", 0),), coarse_spread)
    input_grad = (
        times_transposed(
            grad_wide[2 * coarse_spread : 2 * coarse_spread + half_count], kernels[1][0]
        )
        + times_transposed(coarse_grad, kernels[1][1])
        + times_transposed(grad_wide[0:half_count], kernels[1][2])
    )
    first_grad = upper_rows.astype(jnp.float32) + input_grad * gelu_slope(
        first_pooled.astype(jnp.float32)
    )
    trunk_grad = first_grad * (math.sqrt(windows_total * groups * bin_count) * 0.5)
    lower_grad = (first_grad * 0.5).astype(jnp.bfloat16)
    lower_rows = jnp.repeat(lower_grad, 2, axis=0)
    fine_kernel, fine_mixing, fine_grad = block_backward(
        lower_rows, fine_shifted, fine_inner, fine_gated, mixers[0]
    )
    kernel_terms = jnp.stack([fine_kernel, coarse_kernel])
    mixer_terms = jnp.stack([fine_mixing, coarse_mixing])
    kernel_part, mixer_part, readout_part = (
        lax.psum_scatter(
            kernel_terms.astype(jnp.bfloat16), "seq", scatter_dimension=2, tiled=True
        ).astype(jnp.float32),
        lax.psum_scatter(
            mixer_terms.astype(jnp.bfloat16), "seq", scatter_dimension=1, tiled=True
        ).astype(jnp.float32),
        lax.psum_scatter(
            readout_grad.astype(jnp.bfloat16), "seq", scatter_dimension=0, tiled=True
        ).astype(jnp.float32),
    )
    kernel_total, mixer_total, readout_total = (
        lax.psum_scatter(
            kernel_part.astype(jnp.bfloat16), "dp", scatter_dimension=3, tiled=True
        ).astype(jnp.float32),
        lax.psum_scatter(
            mixer_part.astype(jnp.bfloat16), "dp", scatter_dimension=2, tiled=True
        ).astype(jnp.float32),
        lax.psum_scatter(
            readout_part.astype(jnp.bfloat16), "dp", scatter_dimension=1, tiled=True
        ).astype(jnp.float32),
    )
    return (kernel_total, mixer_total, readout_total, trunk_grad[None])


def solution(mesh):
    placed = (
        P("dp", "seq", None, None),
        P("dp", None, None),
        P("dp"),
        P("dp", "seq", None),
        P("dp", None),
        P(),
        P(),
        P(),
    )
    return jax.shard_map(
        shards,
        mesh=mesh,
        in_specs=placed,
        out_specs=(
            P(None, None, "seq", "dp"),
            P(None, "seq", "dp"),
            P("seq", "dp"),
            P("dp", "seq", None),
        ),
        check_vma=False,
    )
```

profile of v0, /device:TPU:1, one launch (start us, length us, event | category | flops | bytes accessed | tf_op | source)
XLA Modules:
  0.0 1127.8 jit_solution(4078228910551584165)
XLA Ops:
  7.2 0.7 all-gather.2.cloned.1.call-update
  9.8 0.7 fusion.116
  10.5 0.7 fusion.115
  11.2 4.3 compare_select_fusion.2
  15.5 15.7 %fusion.98 = f32[512]{0:T(512)S(1)} fusion(pred[512]{0:T(512)(128)(4,1)S(1)} %compare_reduce_fusion, pred[512]{0:T(512)(128)(4,1)S(1)} %compare_reduce_fusion.1, pred[512]{0:T(512)(128)(4,1)S(1)} %compare_reduce_fusion.2, pred[512]{0:T(512)(128)(4,1)S(1)} %compare_reduce_fusion.3, pred[512]{0:T(512)(128)(4,1)S(1)} %compare_reduce_fusion.4, ...), kind=kLoop, calls=%fused_computation.194 | loop fusion | flops 25600 | bytes 17000 | tf_op jit(solution)/shard_map/convert_element_type | solution.py:102
  31.2 98.4 %all-gather.2.cloned.1.call-done = bf16[8192,768]{1,0:T(8,128)(2,1)} async-done(((bf16[2048,768]{1,0:T(8,128)(2,1)}), bf16[8192,768]{1,0:T(8,128)(2,1)}) %all-gather.2.cloned.1.call-update) | async-done | bytes 12582928 | tf_op jit(solution)/shard_map/all_gather | solution.py:106
  129.6 13.4 %fusion.13 = bf16[512,768]{1,0:T(8,128)(2,1)} fusion(bf16[8192,768]{1,0:T(8,128)(2,1)} %all-gather.2.cloned.1.call-done, bf16[1,1,512,8192]{3,2,1,0:T(8,128)(2,1)} %param.8, f32[512]{0:T(512)S(1)} %fusion.98), kind=kOutput, calls=%fused_computation.29 | convolution fusion | flops 6443237376 | bytes 21760000 | tf_op jit(solution)/shard_map/dot_general | solution.py:104
  143.0 9.2 all-to-all-start
  152.6 14.5 %all-to-all-done = bf16[32,16,768]{2,1,0:T(8,128)(2,1)} async-done(((bf16[32,16,768]{2,1,0:T(8,128)(2,1)}), bf16[32,16,768]{2,1,0:T(8,128)(2,1)}, u32[]{:S(2)}, u32[]{:S(2)}) %all-to-all-start) | async-done | bytes 786464 | tf_op jit(solution)/shard_map/all_to_all | solution.py:111
  167.1 2.6 gather_fusion
  169.8 1.8 fusion.10
  171.6 1.3 collective-permute-start.1
  173.4 4.0 collective-permute-start
  178.0 5.8 collective-permute-done.1
  183.8 0.8 copy-done.28
  185.9 0.9 copy-done.10
  186.8 1.7 convert_add_fusion
  188.6 3.0 reshape.169
  191.6 4.2 reduce_sum.31
  195.7 1.3 fusion.41
  197.1 1.3 collective-permute-start.3
  198.4 4.9 collective-permute-start.2
  203.3 1.4 fusion.55
  204.8 0.7 copy-done.25
  205.5 1.4 fusion.51
  207.0 1.6 fusion.29
  208.6 0.7 copy-done.8
  209.4 1.3 convert_add_fusion.1
  210.6 2.5 reshape.170
  213.1 2.8 reduce_sum.32
  215.9 2.6 fusion.35
  218.6 1.2 fusion.30
  220.1 1.6 fusion.31
  221.8 1.4 fusion.53
  223.2 3.4 collective-permute-start.5
  226.6 1.3 collective-permute-start.4
  228.3 1.5 fusion.49
  229.8 2.9 collective-permute-done.4
  232.7 2.6 multiply_bitcast_fusion
  237.4 2.3 copy.17
  239.8 2.8 convolution_convert_fusion
  242.9 0.6 copy-done.26
  245.0 0.9 copy-done.12
  246.4 0.7 fusion.20
  248.7 0.6 fusion.21
  249.3 0.6 fusion.22
  250.5 5.2 copy.29
  255.7 9.5 reshape.363
  267.1 317.6 %all-reduce.3.cloned.1.call-done = bf16[2,384,768]{2,0,1:T(2,128)(2,1)} async-done(((bf16[2,384,768]{2,0,1:T(2,128)(2,1)}), bf16[2,384,768]{2,0,1:T(2,128)(2,1)}) %all-reduce.3.cloned.1.call-update) | async-done | bytes 1179664
  584.7 0.8 constant_dynamic-slice_fusion
  585.9 0.9 reshape.367
  586.9 243.7 %reduce-scatter.12.cloned.1.call-done = bf16[24,2048]{1,0:T(8,128)(2,1)} async-done(((bf16[768,2048]{1,0:T(8,128)(2,1)}), bf16[24,2048]{1,0:T(8,128)(2,1)}) %reduce-scatter.12.cloned.1.call-update) | async-done | bytes 98320 | tf_op jit(solution)/shard_map/reduce_scatter | solution.py:176
  830.7 229.4 %reduce-scatter.16.cloned.1.call-done = bf16[24,2304]{1,0:T(8,128)(2,1)} async-done(((bf16[768,2304]{1,0:T(8,128)(2,1)}), bf16[24,2304]{1,0:T(8,128)(2,1)}) %reduce-scatter.16.cloned.1.call-update) | async-done | bytes 110608
  1060.1 1.1 reshape.364
  1061.2 1.3 copy.22
  1062.5 2.4 reshape.365
  1064.9 14.0 %reduce-scatter.20.cloned.1.call-done = bf16[192,24]{1,0:T(8,128)(2,1)} async-done(((bf16[768,24]{1,0:T(8,128)(2,1)}), bf16[192,24]{1,0:T(8,128)(2,1)}) %reduce-scatter.20.cloned.1.call-update) | async-done | bytes 9232
  1078.9 0.9 reshape.368
  1079.9 0.6 copy.19
  1080.5 18.3 %reduce-scatter.14.cloned.1.call-done = bf16[24,512]{1,0:T(8,128)(2,1)} async-done(((bf16[24,2048]{1,0:T(8,128)(2,1)}), bf16[24,512]{1,0:T(8,128)(2,1)}) %reduce-scatter.14.cloned.1.call-update) | async-done | bytes 24592 | tf_op jit(solution)/shard_map/reduce_scatter | solution.py:187
  1098.8 1.4 convert_element_type.128
  1100.2 19.0 %reduce-scatter.18.cloned.1.call-done = bf16[96,144]{1,0:T(8,128)(2,1)} async-done(((bf16[384,144]{1,0:T(8,128)(2,1)}), bf16[96,144]{1,0:T(8,128)(2,1)}) %reduce-scatter.18.cloned.1.call-update) | async-done | bytes 27664
  1119.2 1.0 reshape.366
  1120.3 0.6 convert_element_type.125
  (132 shorter events, 13.4 us)
Async XLA Ops:
  7.2 208.8 %copy-start = (bf16[768,2048]{1,0:T(8,128)(2,1)S(1)}, bf16[768,2048]{1,0:T(8,128)(2,1)}, u32[]{:S(2)}) copy-start(bf16[768,2048]{1,0:T(8,128)(2,1)} %param.15) | copy-start | bytes 9437188
  7.2 1.5 copy-start.27
  7.2 122.4 %all-gather.2.cloned.1.call-start = ((), (), s32[]{:S(2)}) async-start(), calls=%async_computation.6 | async-start | bytes 15728640 | tf_op jit(solution)/shard_map/all_gather | solution.py:106
  143.0 24.1 %all-to-all-start = ((bf16[32,16,768]{2,1,0:T(8,128)(2,1)}), bf16[32,16,768]{2,1,0:T(8,128)(2,1)}, u32[]{:S(2)}, u32[]{:S(2)}) async-start(bf16[32,16,768]{2,1,0:T(8,128)(2,1)} %bitcast.145), calls=%async_computation | async-start | bytes 1572864 | tf_op jit(solution)/shard_map/all_to_all | solution.py:111
  152.3 432.4 %all-reduce.3.cloned.1.call-start = ((), (), s32[]{:S(2)}) async-start(), calls=%async_computation.12 | async-start | bytes 2359296
  169.7 3.1 copy-start.4
  169.8 7.6 copy-start.7
  171.5 13.7 %copy-start.5 = (bf16[512,768]{1,0:T(8,128)(2,1)}, bf16[512,768]{1,0:T(8,128)(2,1)S(1)}, u32[]{:S(2)}) copy-start(bf16[512,768]{1,0:T(8,128)(2,1)S(1)} %get-tuple-element.20) | copy-start | bytes 2359300
  171.6 12.2 %collective-permute-start.1 = (bf16[256,768]{1,0:T(8,128)(2,1)S(1)}, bf16[256,768]{1,0:T(8,128)(2,1)S(1)}, u32[]{:S(2)}, u32[]{:S(2)}) collective-permute-start(bf16[256,768]{1,0:T(8,128)(2,1)S(1)} %get-tuple-element.25), channel_id=1, source_target_pairs={{1,0},{2,1},{3,2},{4,3},{5,4},{6,5},{7,6},{8,7},{9,8},{10,9},{11,1... | collective-permute-start | bytes 1179656 | tf_op jit(solution)/shard_map/ppermute | solution.py:20
  173.4 11.8 %collective-permute-start = (bf16[256,768]{1,0:T(8,128)(2,1)S(1)}, bf16[256,768]{1,0:T(8,128)(2,1)S(1)}, u32[]{:S(2)}, u32[]{:S(2)}) collective-permute-start(bf16[256,768]{1,0:T(8,128)(2,1)S(1)} %get-tuple-element.24), channel_id=1, source_target_pairs={{0,1},{1,2},{2,3},{3,4},{4,5},{5,6},{6,7},{7,8},{8,9},{9,10},{10,1... | collective-permute-start | bytes 1179656 | tf_op jit(solution)/shard_map/ppermute | solution.py:19
  183.8 0.8 copy-start.28
  185.2 1.7 copy-start.16
  185.2 0.8 copy-start.23
  185.9 0.9 copy-start.10
  197.1 7.8 collective-permute-start.3
  198.4 8.6 collective-permute-start.2
  204.8 0.7 copy-start.25
  207.0 2.4 copy-start.2
  207.0 2.4 copy-start.17
  207.0 1.6 copy-start.21
  208.6 0.8 copy-start.8
  218.5 1.2 copy-start.13
  220.1 7.8 copy-start.9
  223.2 9.4 copy-start.3
  223.2 5.1 collective-permute-start.5
  226.6 6.0 collective-permute-start.4
  235.3 1.1 copy-start.11
  236.4 0.9 copy-start.19
  237.4 2.4 copy-start.14
  237.4 2.4 copy-start.15
  239.7 590.9 %reduce-scatter.12.cloned.1.call-start = ((), (), s32[]{:S(2)}) async-start(), calls=%async_computation.7 | async-start | bytes 3244032 | tf_op jit(solution)/shard_map/reduce_scatter | solution.py:176
  242.6 0.9 copy-start.26
  242.6 1.3 copy-start.22
  242.6 817.5 %reduce-scatter.16.cloned.1.call-start = ((), (), s32[]{:S(2)}) async-start(), calls=%async_computation.9 | async-start | bytes 3649536
  244.7 1.1 copy-start.12
  244.7 1.5 copy-start.18
  244.7 1.7 copy-start.20
  246.4 1.1 copy-start.6
  246.4 1.2 copy-start.29
  247.7 1.0 copy-start.24
  265.2 0.7 copy-start.30
  265.3 813.6 %reduce-scatter.20.cloned.1.call-start = ((), (), s32[]{:S(2)}) async-start(), calls=%async_computation.11 | async-start | bytes 245760
  586.8 512.0 %reduce-scatter.14.cloned.1.call-start = ((), (), s32[]{:S(2)}) async-start(), calls=%async_computation.8 | async-start | bytes 122880 | tf_op jit(solution)/shard_map/reduce_scatter | solution.py:187
  830.6 288.6 %reduce-scatter.18.cloned.1.call-start = ((), (), s32[]{:S(2)}) async-start(), calls=%async_computation.10 | async-start | bytes 245760
  1060.1 60.9 %copy-start.1 = (bf16[768,2048]{1,0:T(8,128)(2,1)S(1)}, bf16[768,2048]{1,0:T(8,128)(2,1)}, u32[]{:S(2)}) copy-start(bf16[768,2048]{1,0:T(8,128)(2,1)} %param.15) | copy-start | bytes 9437188
Sparse Core Ops, SparseCore 0:
  9.7 119.8 all-gather.1
  239.9 344.7 all-reduce.2
  590.4 240.1 reduce-scatter.11
  836.2 223.8 reduce-scatter.15
  1062.4 16.4 reduce-scatter.19
  1081.1 17.6 reduce-scatter.13
  1101.3 17.8 reduce-scatter.17
where the time goes:
time: 1130 us
  waiting for transfers between devices  965 us (85%)
  local copies, waits for them, and re-layouts  45.9 us (4%)
  matrix products  40.8 us (4%)
  other arithmetic  34.5 us (3%)
  starting transfers between devices  25.9 us (2%)
  between operations  16.2 us (1%)
    unnamed x11, waiting for transfers between devices  581 us
    reduce_scatter x1, waiting for transfers between devices, shards(): lax.psum_scatter(readout_grad.astype(jnp.bfloat16), 'seq', scatter_dimens...  244 us
    all_gather x1, waiting for transfers between devices, shards(): lax.all_gather(projection, 'dp', axis=0, tiled=True)  98.4 us
    unnamed x76, local copies, waits for them, and re-layouts  32.6 us
  transfers between devices with their start and end apart: 14, of which 11 were waited for; matrix products, arithmetic and copies ran while one was open for 5% of the time, Pallas kernels for 0%

commit v1 on v0

--- a/solution.py
+++ b/solution.py
@@ -3,10 +3,374 @@
 import jax
 import jax.numpy as jnp
 from jax import lax
+from jax.experimental import pallas as pl
+from jax.experimental.pallas import tpu as pltpu
 from jax.sharding import PartitionSpec as P
 
 SPREAD_FINE = 256
 SPREAD_COARSE = 128
+MESH = pl.DeviceIdType.MESH
+CHUNK = 512
+ORDERS = ((0, 1, 2), (1, 2, 0), (2, 0, 1))
+WIDTHS = (384, 384, 512)
+
+
+def place():
+    dp, seq = lax.axis_index("dp"), lax.axis_index("seq")
+    core = lax.rem(dp, 2)
+    x = lax.rem(lax.div(seq, 4), 2) * 2 + lax.div(dp, 2)
+    return (x, lax.div(seq, 8), lax.rem(seq, 4)), core
+
+
+def device_at(coords, core):
+    x, y, z = coords
+    return (lax.rem(x, 2) * 2 + core, y * 8 + lax.div(x, 2) * 4 + z)
+
+
+def moved(coords, axis, step):
+    out = list(coords)
+    out[axis] = lax.rem(out[axis] + step, 4)
+    return tuple(out)
+
+
+class Sender:
+    def __init__(self, send_sems, recv_sems):
+        self.send_sems, self.recv_sems, self.copies = send_sems, recv_sems, []
+
+    def __call__(self, src, dst, device):
+        at = len(self.copies)
+        copy = pltpu.make_async_remote_copy(
+            src_ref=src,
+            dst_ref=dst,
+            send_sem=self.send_sems.at[at],
+            recv_sem=self.recv_sems.at[at],
+            device_id=device,
+            device_id_type=MESH,
+        )
+        copy.start()
+        self.copies.append(copy)
+        return copy
+
+    def finish(self):
+        for copy in self.copies:
+            copy.wait_send()
+
+
+def greet(devices):
+    barrier = pltpu.get_barrier_semaphore()
+    for device in devices:
+        pl.semaphore_signal(barrier, inc=1, device_id=device, device_id_type=MESH)
+    pl.semaphore_wait(barrier, len(devices))
+
+
+def f32(values):
+    return values.astype(jnp.float32)
+
+
+def project_kernel(emb, weights, out, emb_v, w_v, acc, rows_v, landed, local_sems, send_sems, recv_sems, a2a_send, a2a_recv):
+    coords, core = place()
+    dp, seq = lax.axis_index("dp"), lax.axis_index("seq")
+    groups = lax.axis_size("seq")
+    depth = weights.shape[0]
+    partner = device_at(coords, 1 - core)
+    up, down = device_at(moved(coords, 0, 1), core), device_at(moved(coords, 0, 3), core)
+    across = lax.rem(dp + 2, 4)
+    order = (dp, dp + 1 - 2 * core, across, across + 1 - 2 * core)
+    own_w = pltpu.make_async_copy(weights, w_v.at[dp], local_sems.at[4])
+    own_w.start()
+    loads = []
+    for at, quarter in enumerate(order):
+        cols = pl.ds(pl.multiple_of(quarter * depth, depth), depth)
+        load = pltpu.make_async_copy(emb.at[:, cols], emb_v.at[:, cols], local_sems.at[at])
+        load.start()
+        loads.append(load)
+
+    barrier = pltpu.get_barrier_semaphore()
+
+    @pl.loop(1, groups)
+    def _(off):
+        pl.semaphore_signal(
+            barrier, inc=1, device_id=(dp, lax.rem(seq + off, groups)), device_id_type=MESH
+        )
+
+    for device in (partner, up, down):
+        pl.semaphore_signal(barrier, inc=1, device_id=device, device_id_type=MESH)
+    pl.semaphore_wait(barrier, groups + 2)
+
+    send = Sender(send_sems, recv_sems)
+    crossing = []
+    for part in range(2):
+        for side, device in enumerate((up, down)):
+            rows = pl.ds(side * (depth // 2) + part * CHUNK, CHUNK)
+            crossing.append(send(weights.at[rows], w_v.at[dp, rows], device))
+    to_partner = send(weights, w_v.at[dp], partner)
+
+    def accumulate(quarter, row):
+        cols = pl.ds(pl.multiple_of(quarter * depth + row, CHUNK), CHUNK)
+        acc[...] += jnp.dot(
+            emb_v[:, cols],
+            w_v[quarter, pl.ds(pl.multiple_of(row, CHUNK), CHUNK), :],
+            preferred_element_type=jnp.float32,
+        )
+
+    acc[...] = jnp.zeros_like(acc)
+    loads[0].wait()
+    own_w.wait()
+
+    @pl.loop(0, depth // CHUNK)
+    def _(step):
+        accumulate(order[0], step * CHUNK)
+
+    loads[1].wait()
+    to_partner.wait_recv()
+
+    @pl.loop(0, depth // CHUNK)
+    def _(step):
+        accumulate(order[1], step * CHUNK)
+
+    loads[2].wait()
+    loads[3].wait()
+    relays = []
+    for at, copy in enumerate(crossing):
+        copy.wait_recv()
+        row = (at % 2) * (depth // 2) + (at // 2) * CHUNK
+        block = w_v.at[across, pl.ds(row, CHUNK)]
+        relays.append(send(block, block, partner))
+        accumulate(across, row)
+    for at, copy in enumerate(relays):
+        copy.wait_recv()
+        accumulate(order[3], (at % 2) * (depth // 2) + (at // 2) * CHUNK)
+
+    block_rows = rows_v.shape[1]
+    rows_v[...] = acc[...].astype(jnp.bfloat16).reshape(rows_v.shape)
+
+    def block_copy(off):
+        there = lax.rem(seq + off, groups)
+        return pltpu.make_async_remote_copy(
+            src_ref=rows_v.at[there],
+            dst_ref=landed.at[seq],
+            send_sem=a2a_send.at[off],
+            recv_sem=a2a_recv.at[off],
+            device_id=(dp, there),
+            device_id_type=MESH,
+        )
+
+    @pl.loop(1, groups)
+    def _(off):
+        block_copy(off).start()
+
+    landed[seq] = rows_v[seq]
+
+    @pl.loop(1, groups)
+    def _(off):
+        block_copy(off).wait()
+
+    send.finish()
+    out[...] = landed[...]
+
+
+def project_and_exchange(emb, weights):
+    rows, emb_width = emb.shape
+    depth, channels = weights.shape
+    groups = lax.axis_size("seq")
+    blocks = (groups, rows // groups, channels)
+    n_copies = 9
+    return pl.pallas_call(
+        project_kernel,
+        out_shape=jax.ShapeDtypeStruct(blocks, jnp.bfloat16),
+        in_specs=[pl.BlockSpec(memory_space=pl.ANY)] * 2,
+        out_specs=pl.BlockSpec(memory_space=pltpu.VMEM),
+        scratch_shapes=[
+            pltpu.VMEM((rows, emb_width), jnp.bfloat16),
+            pltpu.VMEM((4, depth, channels), jnp.bfloat16),
+            pltpu.VMEM((rows, channels), jnp.float32),
+            pltpu.VMEM(blocks, jnp.bfloat16),
+            pltpu.VMEM(blocks, jnp.bfloat16),
+            pltpu.SemaphoreType.DMA((5,)),
+            pltpu.SemaphoreType.DMA((n_copies,)),
+            pltpu.SemaphoreType.DMA((n_copies,)),
+            pltpu.SemaphoreType.DMA((groups,)),
+            pltpu.SemaphoreType.DMA((groups,)),
+        ],
+        compiler_params=pltpu.CompilerParams(
+            collective_id=0, has_side_effects=True, vmem_limit_bytes=56 << 20
+        ),
+        name="project",
+    )(emb, weights)
+
+
+class Part:
+    def __init__(self, order, terms, scratch, send, coords, core):
+        self.order, self.terms, self.send, self.coords, self.core = order, terms, send, coords, core
+        (self.pair, self.acc1, self.halves1, self.acc2, self.halves2, self.acc3, self.last) = scratch
+
+    def start_pair(self):
+        self.pair_copy = self.send(
+            self.terms.at[1 - self.core], self.pair, device_at(self.coords, 1 - self.core)
+        )
+
+    def end_pair(self):
+        self.pair_copy.wait_recv()
+
+        @pl.loop(0, 4)
+        def _(at):
+            self.acc1[at] = (f32(self.terms[self.core, at]) + f32(self.pair[at])).astype(jnp.bfloat16)
+
+    def level(self, number):
+        acc, halves = (self.acc1, self.halves1) if number == 0 else (self.acc2, self.halves2)
+        axis = self.order[number]
+        here = self.coords[axis]
+        up, down = (device_at(moved(self.coords, axis, k), self.core) for k in (1, 3))
+        return acc, halves, here, up, down
+
+    def start_level(self, number):
+        acc, halves, here, up, down = self.level(number)
+        after, before, opposite = (lax.rem(here + k, 4) for k in (1, 3, 2))
+        low, high = pl.ds(0, 2), pl.ds(2, 2)
+        self.arrivals = [
+            self.send(acc.at[opposite, low], halves.at[0], up),
+            self.send(acc.at[opposite, high], halves.at[1], down),
+            self.send(acc.at[before, low], halves.at[2], down),
+            self.send(acc.at[after, high], halves.at[3], up),
+        ]
+
+    def relay_level(self, number):
+        acc, halves, here, up, down = self.level(number)
+        after, before = (lax.rem(here + k, 4) for k in (1, 3))
+        self.arrivals[0].wait_recv()
+        halves[4] = (f32(halves[0]) + f32(acc[after, 0:2])).astype(jnp.bfloat16)
+        self.arrivals.append(self.send(halves.at[4], halves.at[6], up))
+        self.arrivals[1].wait_recv()
+        halves[5] = (f32(halves[1]) + f32(acc[before, 2:4])).astype(jnp.bfloat16)
+        self.arrivals.append(self.send(halves.at[5], halves.at[7], down))
+
+    def end_level(self, number):
+        acc, halves, here, _, _ = self.level(number)
+        into = self.acc2 if number == 0 else self.acc3
+        for copy in self.arrivals[2:]:
+            copy.wait_recv()
+        into[0:2] = (f32(acc[here, 0:2]) + f32(halves[2]) + f32(halves[6])).astype(jnp.bfloat16)
+        into[2:4] = (f32(acc[here, 2:4]) + f32(halves[3]) + f32(halves[7])).astype(jnp.bfloat16)
+
+    def start_last(self):
+        axis = self.order[2]
+        here = self.coords[axis]
+        self.arrivals = [
+            self.send(
+                self.acc3.at[lax.rem(here + k, 4)],
+                self.last.at[k - 1],
+                device_at(moved(self.coords, axis, k), self.core),
+            )
+            for k in (1, 2, 3)
+        ]
+
+    def end_last(self):
+        here = self.coords[self.order[2]]
+        for copy in self.arrivals:
+            copy.wait_recv()
+        return f32(self.acc3[here]) + f32(self.last[0]) + f32(self.last[1]) + f32(self.last[2])
+
+
+N_REDUCE = 3 * (1 + 6 + 6 + 3) + 3
+
+
+def reduce_kernel(terms0, terms1, terms2, kernel_out, mixer_out, readout_out, *scratch):
+    parts_scratch, (joined, send_sems, recv_sems) = scratch[:-3], scratch[-3:]
+    coords, core = place()
+    dp = lax.axis_index("dp")
+    send = Sender(send_sems, recv_sems)
+    parts = [
+        Part(ORDERS[at], terms, parts_scratch[7 * at : 7 * at + 7], send, coords, core)
+        for at, terms in enumerate((terms0, terms1, terms2))
+    ]
+    pair_x = (coords[0] + 1 - 2 * lax.rem(coords[0], 2),) + coords[1:]
+    partner = device_at(coords, 1 - core)
+    group = [partner, device_at(pair_x, core), device_at(pair_x, 1 - core)]
+    greet(
+        [device_at(moved(coords, axis, k), core) for axis in range(3) for k in (1, 2, 3)]
+        + [partner, device_at(pair_x, 1 - core)]
+    )
+    for part in parts:
+        part.start_pair()
+    for part in parts:
+        part.end_pair()
+        part.start_level(0)
+    for part in parts:
+        part.relay_level(0)
+    for part in parts:
+        part.end_level(0)
+        part.start_level(1)
+    for part in parts:
+        part.relay_level(1)
+    for part in parts:
+        part.end_level(1)
+        part.start_last()
+    joined[dp, :, 0:384] = parts[0].end_last()
+    joined[dp, :, 384:768] = parts[1].end_last()
+    mine = joined.at[dp]
+    last = [send(mine, mine, device) for device in group]
+    readout_out[...] = parts[2].end_last()
+    for copy in last:
+        copy.wait_recv()
+    for index in range(4):
+
+        @pl.when(dp == index)
+        def _():
+            low = 96 * index
+            for tap in range(6):
+                slot, start = (tap, low) if tap < 4 else (tap - 4, 384 + low)
+                kernel_out[tap] = joined[slot, :, start : start + 96]
+            slot, start = 2 + index // 2, 384 + 192 * (index % 2)
+            mixer_out[0] = joined[slot, 0:12, start : start + 192]
+            mixer_out[1] = joined[slot, 12:24, start : start + 192]
+
+    send.finish()
+
+
+def part_scratch(width):
+    unit = (24, width)
+    return [
+        pltpu.VMEM(shape + unit, jnp.bfloat16)
+        for shape in ((4, 4, 4), (4, 4, 4), (8, 2, 4), (4, 4), (8, 2), (4,), (3,))
+    ]
+
+
+def reduce_terms(terms):
+    vmem = pl.BlockSpec(memory_space=pltpu.VMEM)
+    return pl.pallas_call(
+        reduce_kernel,
+        out_shape=(
+            jax.ShapeDtypeStruct((6, 24, 96), jnp.float32),
+            jax.ShapeDtypeStruct((2, 12, 192), jnp.float32),
+            jax.ShapeDtypeStruct((24, 512), jnp.float32),
+        ),
+        in_specs=[vmem] * 3,
+        out_specs=[vmem] * 3,
+        scratch_shapes=[s for width in WIDTHS for s in part_scratch(width)]
+        + [
+            pltpu.VMEM((4, 24, 768), jnp.float32),
+            pltpu.SemaphoreType.DMA((N_REDUCE,)),
+            pltpu.SemaphoreType.DMA((N_REDUCE,)),
+        ],
+        compiler_params=pltpu.CompilerParams(
+            collective_id=2, has_side_effects=True, vmem_limit_bytes=56 << 20
+        ),
+        name="reduce_gradients",
+    )(*terms)
+
+
+def arrange_terms(kernel_terms, mixer_terms, readout_terms):
+    bf16 = jnp.bfloat16
+    kernels = kernel_terms.astype(bf16).reshape(6, 768, 384)
+    mixers = mixer_terms.astype(bf16).reshape(2, 32, 12, 768).transpose(1, 0, 2, 3).reshape(768, 2, 384)
+    first = kernels[:4].reshape(2, 2, 4, 2, 4, 24, 384)
+    second = jnp.concatenate([kernels[4:], mixers.transpose(1, 0, 2)]).reshape(2, 2, 4, 2, 4, 24, 384)
+    third = readout_terms.astype(bf16).reshape(4, 2, 4, 24, 2, 2, 512).transpose(4, 5, 0, 1, 2, 3, 6)
+    return (
+        first.transpose(1, 3, 0, 2, 4, 5, 6).reshape(2, 4, 4, 4, 24, 384),
+        second.transpose(1, 2, 4, 3, 0, 5, 6).reshape(2, 4, 4, 4, 24, 384),
+        third.transpose(1, 4, 3, 0, 2, 5, 6).reshape(2, 4, 4, 4, 24, 512),
+    )
 
 
 def with_halo(shard, sides, width):
@@ -91,31 +455,10 @@
     own_column = lax.dynamic_index_in_dim(layout_table, device, axis=1, keepdims=False)
     matches = (own_column[:, None] == shard_ids[None, :]).astype(jnp.int32)
     source_index = jnp.sum(shard_ids[:, None] * matches, axis=0)
-    row_ids = jnp.arange(row_count, dtype=jnp.int32)
-    owner_shard = row_ids // block_rows
-    own_slots = lax.dynamic_index_in_dim(layout_table, device, axis=0, keepdims=False)
-    source_position = (
-        owner_shard * row_count
-        + jnp.take(own_slots, owner_shard) * block_rows
-        + row_ids % block_rows
-    )
-    inside = (source_position < length).astype(jnp.float32)
-    outgoing = (
-        jnp.dot(
-            local_rows,
-            lax.all_gather(projection, "dp", axis=0, tiled=True),
-            preferred_element_type=jnp.float32,
-        )
-        * inside[:, None]
-    ).astype(jnp.bfloat16)
-    received = lax.all_to_all(
-        outgoing.reshape(groups, block_rows, channels),
-        "seq",
-        split_axis=0,
-        concat_axis=0,
-        tiled=True,
-    )
+    received = project_and_exchange(local_rows, projection)
     hidden = jnp.take(received, source_index, axis=0).reshape(row_count, channels)
+    positions = device * row_count + jnp.arange(row_count, dtype=jnp.int32)
+    hidden = jnp.where((positions < length)[:, None], hidden, jnp.zeros_like(hidden))
     fine_spread = SPREAD_FINE
     coarse_spread = SPREAD_COARSE
     half_count = row_count // 2
@@ -166,29 +509,10 @@
     )
     kernel_terms = jnp.stack([fine_kernel, coarse_kernel])
     mixer_terms = jnp.stack([fine_mixing, coarse_mixing])
-    kernel_part, mixer_part, readout_part = (
-        lax.psum_scatter(
-            kernel_terms.astype(jnp.bfloat16), "seq", scatter_dimension=2, tiled=True
-        ).astype(jnp.float32),
-        lax.psum_scatter(
-            mixer_terms.astype(jnp.bfloat16), "seq", scatter_dimension=1, tiled=True
-        ).astype(jnp.float32),
-        lax.psum_scatter(
-            readout_grad.astype(jnp.bfloat16), "seq", scatter_dimension=0, tiled=True
-        ).astype(jnp.float32),
-    )
-    kernel_total, mixer_total, readout_total = (
-        lax.psum_scatter(
-            kernel_part.astype(jnp.bfloat16), "dp", scatter_dimension=3, tiled=True
-        ).astype(jnp.float32),
-        lax.psum_scatter(
-            mixer_part.astype(jnp.bfloat16), "dp", scatter_dimension=2, tiled=True
-        ).astype(jnp.float32),
-        lax.psum_scatter(
-            readout_part.astype(jnp.bfloat16), "dp", scatter_dimension=1, tiled=True
-        ).astype(jnp.float32),
-    )
-    return (kernel_total, mixer_total, readout_total, trunk_grad[None])
+    kernel_total, mixer_total, readout_total = reduce_terms(
+        arrange_terms(kernel_terms, mixer_terms, readout_grad)
+    )
+    return (kernel_total.reshape(2, 3, 24, 96), mixer_total, readout_total, trunk_grad[None])
 
 
 def solution(mesh):

time: 1130 us -> 246 us (0.22)
  waiting for transfers between devices: 965 us -> 10.4 us
  Pallas kernels: 0 us -> 116 us
  other arithmetic: 34.5 us -> 12.7 us
  between operations: 16.2 us -> 1.79 us
    unnamed x11 -> x0, waiting for transfers between devices: 581 us -> none
    reduce_scatter x2 -> x0, waiting for transfers between devices: 262 us -> none  [the longest x1 244 us: shards(): lax.psum_scatter(readout_grad.astype(jnp.bfloat16), 'seq', scatter_dimens...]
    pallas_call x0 -> x2, Pallas kernels: none -> 116 us  [the longest x1 62.2 us: project_and_exchange(): pl.pallas_call(project_kernel, out_shape=jax.ShapeDtypeStruct(blocks, jnp...]
    all_gather x1 -> x0, waiting for transfers between devices: 98.4 us -> none  [shards(): lax.all_gather(projection, 'dp', axis=0, tiled=True)]
    unnamed x76 -> x69, local copies, waits for them, and re-layouts: 32.6 us -> 9.42 us
    convert_element_type x3 -> x0, other arithmetic: 17.7 us -> none  [the longest x1 15.7 us: shards(): inside = (source_position < length).astype(jnp.float32)]
    all_to_all x1 -> x0, waiting for transfers between devices: 14.5 us -> none  [shards(): lax.all_to_all(outgoing.reshape(groups, block_rows, channels), 'seq', spl...]
    dot_general x1 -> x0, matrix products: 13.4 us -> none  [shards(): jnp.dot(local_rows, lax.all_gather(projection, 'dp', axis=0, tiled=True),...]
  transfers between devices with their start and end apart: 14 -> 6, of which waited for: 11 -> 2; matrix products, arithmetic and copies ran while one was open for 5% -> 8% of each run, Pallas kernels for 0% -> 0%
where the time goes in v1:
time: 246 us; the launch traced here: 245 us
  Pallas kernels  116 us (47%)
  local copies, waits for them, and re-layouts  45.3 us (18%)
  matrix products  39.8 us (16%)
  starting transfers between devices  19.2 us (8%)
  other arithmetic  12.7 us (5%)
  waiting for transfers between devices  10.4 us (4%)
    pallas_call x1, Pallas kernels, project_and_exchange(): pl.pallas_call(project_kernel, out_shape=jax.ShapeDtypeStruct(blocks, jnp...  62.2 us
    pallas_call x1, Pallas kernels, reduce_terms(): pl.pallas_call(reduce_kernel, out_shape=(jax.ShapeDtypeStruct((6, 24, 96)...  53.5 us
    dot_general x9, matrix products, matmul(): return jnp.dot(left_side, right_side, preferred_element_type=jnp.float32)  19.2 us
    ppermute x3, starting transfers between devices, with_halo(): before = lax.ppermute(last, axis, up)  15.1 us
    ppermute x3, waiting for transfers between devices, with_halo(): after = lax.ppermute(leading, axis, down)  10.4 us
    dot_general x6, matrix products, times_transposed(): lax.dot_general(left_side, right_side, (((1,), (1,)), ((), ())), preferre...  10.4 us
    dot_general x9, matrix products, transposed_times(): lax.dot_general(left_side, right_side, (((0,), (0,)), ((), ())), preferre...  10.2 us
    unnamed x69, local copies, waits for them, and re-layouts  9.42 us
  transfers between devices with their start and end apart: 6, of which 2 were waited for; matrix products, arithmetic and copies ran while one was open for 8% of the time, Pallas kernels for 0%

profile of v1, /device:TPU:1, one launch (start us, length us, event | category | flops | bytes accessed | tf_op | source)
XLA Modules:
  0.0 244.9 jit_solution(13056286848038518599)
XLA Ops:
  0.7 1.0 dynamic-slice_reduce_fusion
  2.7 62.2 %project.1 = bf16[32,16,768]{2,1,0:T(8,128)(2,1)} custom-call(bf16[512,8192]{1,0:T(8,128)(2,1)} %bitcast.127, bf16[2048,768]{1,0:T(8,128)(2,1)} %weights.1), custom_call_target="tpu_custom_call" | custom-call | tf_op jit(solution)/shard_map/project/pallas_call | solution.py:178
  64.8 2.6 %gather_fusion = bf16[32,16,768]{2,1,0:T(8,128)(2,1)} fusion(bf16[32,16,768]{2,1,0:T(8,128)(2,1)} %project.1, s32[1024]{0:T(1024)S(1)} %pad_clamp_fusion), kind=kCustom, calls=%fused_computation | custom fusion | bytes 1572992 | tf_op jit(solution)/shard_map/jit(_take)/gather | solution.py:459
  67.5 2.5 %fusion.5 = (bf16[512,768]{1,0:T(8,128)(2,1)S(1)}, bf16[512,768]{1,0:T(8,128)(2,1)}) fusion(bf16[32,16,768]{2,1,0:T(8,128)(2,1)} %gather_fusion, pred[512]{0:T(512)(128)(4,1)S(1)} %broadcast_in_dim.49, pred[512]{0:T(512)(128)(4,1)S(1)} %add_compare_fusion.1), kind=kLoop, calls=%fused_computation.23 | loop fusion | flops 3145728 | bytes 2360320 | tf_op jit(solution)/shard_map/convert_element_type | solution.py:465
  70.0 0.9 copy-done.4
  70.8 0.8 fusion.95
  71.7 3.9 %collective-permute-start = (bf16[256,768]{1,0:T(8,128)(2,1)S(1)}, bf16[256,768]{1,0:T(8,128)(2,1)}, u32[]{:S(2)}, u32[]{:S(2)}) collective-permute-start(bf16[256,768]{1,0:T(8,128)(2,1)S(1)} %get-tuple-element.26), channel_id=1, source_target_pairs={{0,1},{1,2},{2,3},{3,4},{4,5},{5,6},{6,7},{7,8},{8,9},{9,10},{10,1... | collective-permute-start | bytes 1179656 | tf_op jit(solution)/shard_map/ppermute | solution.py:383
  75.6 1.3 collective-permute-start.1
  76.9 0.5 fusion.1
  77.4 2.5 %fusion.56 = f32[512,384]{0,1:T(8,128)} fusion(bf16[512,768]{1,0:T(8,128)(2,1)S(1)} %bitcast.130, bf16[2,3,768,384]{3,2,1,0:T(8,128)(2,1)} %param.13), kind=kOutput, calls=%fused_computation.100 | convolution fusion | flops 301989888 | bytes 2162688 | tf_op jit(solution)/shard_map/dot_general | solution.py:400
  79.9 6.9 %collective-permute-done.1 = bf16[256,768]{1,0:T(8,128)(2,1)} collective-permute-done((bf16[256,768]{1,0:T(8,128)(2,1)}, bf16[256,768]{1,0:T(8,128)(2,1)}, u32[]{:S(2)}, u32[]{:S(2)}) %collective-permute-start.1) | collective-permute-done | bytes 393248 | tf_op jit(solution)/shard_map/ppermute | solution.py:384
  86.8 1.8 fusion.54
  88.6 2.7 %multiply_convert_fusion.2 = (bf16[512,384]{0,1:T(8,128)(2,1)S(1)}, f32[512,384]{0,1:T(8,128)}) fusion(f32[512,384]{0,1:T(8,128)S(1)} %fusion.54, f32[512,384]{0,1:T(8,128)S(1)} %copy-done.13, bf16[2,3,768,384]{3,2,1,0:T(8,128)(2,1)} %param.13, bf16[512,768]{1,0:T(8,128)(2,1)S(1)} %copy-done.5, bf16[256,768]{1,0:T(8,128)(2,1)} %collective-permute-done), kind=kOutput, calls=%fused_computation.81 | convolution fusion | flops 304939008 | bytes 4521984 | tf_op jit(solution)/shard_map/dot_general | solution.py:400
  91.3 0.9 reshape.175
  92.2 3.1 %convert_add_fusion = f32[512,768]{1,0:T(8,128)} fusion(bf16[512,768]{1,0:T(8,128)(2,1)} %get-tuple-element.23, bf16[512,384]{0,1:T(8,128)(2,1)S(1)} %get-tuple-element.32, bf16[2,384,768]{2,1,0:T(8,128)(2,1)} %param.14), kind=kOutput, calls=%fused_computation.4 | convolution fusion | flops 302776320 | bytes 3342336 | tf_op jit(solution)/shard_map/dot_general | solution.py:400
  95.3 3.0 %reshape.169 = f32[256,2,768]{2,1,0:T(2,128)} reshape(f32[512,768]{1,0:T(8,128)} %convert_add_fusion) | data formatting | bytes 3145728 | tf_op jit(solution)/shard_map/reshape | solution.py:431
  98.3 4.2 %reduce_sum.31 = f32[256,768]{1,0:T(8,128)} reduce(f32[256,2,768]{2,1,0:T(2,128)} %reshape.169, f32[]{:T(128)} %constant.31.clone.1), dimensions={1}, to_apply=%region_1.2 | reduce | flops 196608 | bytes 2359300 | tf_op jit(solution)/shard_map/reduce_sum | solution.py:431
  102.5 1.3 fusion.33
  103.8 4.7 %collective-permute-start.2 = (bf16[128,768]{1,0:T(8,128)(2,1)S(1)}, bf16[128,768]{1,0:T(8,128)(2,1)S(1)}, u32[]{:S(2)}, u32[]{:S(2)}) collective-permute-start(bf16[128,768]{1,0:T(8,128)(2,1)S(1)} %get-tuple-element.28), channel_id=1, source_target_pairs={{0,1},{1,2},{2,3},{3,4},{4,5},{5,6},{6,7},{7,8},{8,9},{9,10},{10,1... | collective-permute-start | bytes 589832 | tf_op jit(solution)/shard_map/ppermute | solution.py:383
  108.5 1.5 collective-permute-start.3
  110.0 1.4 fusion.48
  111.4 3.5 %collective-permute-done.3 = bf16[128,768]{1,0:T(8,128)(2,1)S(1)} collective-permute-done((bf16[128,768]{1,0:T(8,128)(2,1)S(1)}, bf16[128,768]{1,0:T(8,128)(2,1)S(1)}, u32[]{:S(2)}, u32[]{:S(2)}) %collective-permute-start.3) | collective-permute-done | bytes 196640 | tf_op jit(solution)/shard_map/ppermute | solution.py:384
  115.0 0.7 copy-done.31
  115.6 1.4 fusion.44
  117.1 2.4 multiply_convert_fusion.4
  119.4 0.7 copy-done.18
  120.1 1.3 convert_add_fusion.1
  121.4 2.5 %reshape.170 = f32[128,2,768]{2,1,0:T(2,128)} reshape(f32[256,768]{1,0:T(8,128)} %convert_add_fusion.1) | data formatting | bytes 1572864 | tf_op jit(solution)/shard_map/reshape | solution.py:431
  123.9 2.8 %reduce_sum.32 = f32[128,768]{1,0:T(8,128)} reduce(f32[128,2,768]{2,1,0:T(2,128)} %reshape.170, f32[]{:T(128)} %constant.31.clone.1), dimensions={1}, to_apply=%region_2.3 | reduce | flops 98304 | bytes 1179652 | tf_op jit(solution)/shard_map/reduce_sum | solution.py:431
  126.7 2.6 %fusion.27 = bf16[128,2048]{1,0:T(8,128)(2,1)S(1)} fusion(s32[1,128,2048]{2,1,0:T(8,128)} %param.11, f32[128]{0:T(128)S(1)} %compare_select_fusion.3, bf16[768,2048]{1,0:T(8,128)(2,1)S(1)} %copy-done, f32[128,768]{1,0:T(8,128)} %reduce_sum.32), kind=kOutput, calls=%fused_computation.62 | convolution fusion | flops 406519808 | bytes 5112320 | tf_op jit(solution)/shard_map/dot_general | solution.py:400
  129.4 1.2 fusion.22
  130.9 0.9 reshape.192
  132.5 0.7 fusion.97
  133.2 1.2 fusion.18
  134.4 2.4 fusion.46
  136.8 2.6 %convolution_convert_fusion = bf16[768,2048]{1,0:T(8,128)(2,1)} fusion(bf16[128,2048]{1,0:T(8,128)(2,1)S(1)} %copy-done.17, f32[128,768]{1,0:T(8,128)S(1)} %copy-done.24), kind=kOutput, calls=%fused_computation.2 | convolution fusion | flops 404422656 | bytes 4063232 | tf_op jit(solution)/shard_map/dot_general | solution.py:410
  139.6 0.7 reshape.176
  140.3 1.3 collective-permute-start.4
  141.6 6.5 %collective-permute-start.5 = (bf16[128,384]{1,0:T(8,128)(2,1)}, bf16[128,384]{1,0:T(8,128)(2,1)}, u32[]{:S(2)}, u32[]{:S(2)}) collective-permute-start(bf16[128,384]{1,0:T(8,128)(2,1)} %get-tuple-element.31), channel_id=1, source_target_pairs={{0,1},{1,2},{2,3},{3,4},{4,5},{5,6},{6,7},{7,8},{8,9},{9,10},{10,1... | collective-permute-start | bytes 294920 | tf_op jit(solution)/shard_map/ppermute | solution.py:383
  148.2 4.8 %reshape.180 = bf16[4,2,4,24,2,2,512]{6,5,4,3,2,1,0:T(2,128)(2,1)S(1)} reshape(bf16[768,2048]{1,0:T(8,128)(2,1)} %convolution_convert_fusion) | data formatting | bytes 6291456 | tf_op jit(solution)/shard_map/reshape | solution.py:368
  153.0 2.4 copy.35
  156.7 0.8 copy-done.23
  157.5 1.1 fusion.20
  158.7 1.5 fusion.42
  160.2 2.6 %multiply_bitcast_fusion = (f32[1,256,768]{2,1,0:T(8,128)}, bf16[256,768]{1,0:T(8,128)(2,1)S(1)}) fusion(f32[256,768]{1,0:T(8,128)S(1)} %copy-done.3, f32[256,768]{1,0:T(8,128)S(1)} %fusion.42, f32[256,768]{1,0:T(8,128)S(1)} %copy-done.11, bf16[2,3,768,384]{3,2,1,0:T(8,128)(2,1)} %param.13, bf16[128,384]{1,0:T(8,128)(2,1)} %collective-permute-done.4, ...), kind=kOutput, calls=%fused_computation.78 | convolution fusion | flops 155123712 | bytes 4816896 | tf_op jit(solution)/shard_map/dot_general | solution.py:404
  163.3 1.2 reshape.191
  164.5 1.2 reshape.172
  165.7 2.3 fusion.12
  168.0 0.6 fusion.14
  168.6 1.6 fusion.15
  170.2 1.6 fusion.13
  172.5 1.2 slice.125
  173.9 0.9 copy-done.12
  174.9 0.6 fusion.16
  175.5 0.4 copy-done.15
  176.1 1.8 copy.32
  177.9 3.9 %reshape.177 = bf16[768,2,384]{2,1,0:T(2,128)(2,1)} reshape(bf16[32,2,12,768]{3,2,1,0:T(8,128)(2,1)} %copy.32) | data formatting | bytes 2359296 | tf_op jit(solution)/shard_map/reshape | solution.py:365
  181.8 1.4 copy.43
  183.3 1.8 copy.28
  185.3 1.7 copy.34
  187.0 53.5 %reduce_gradients.1 = (f32[6,24,96]{2,1,0:T(8,128)}, f32[2,12,192]{2,1,0:T(8,128)}, f32[24,512]{1,0:T(8,128)}) custom-call(bf16[2,4,4,4,24,384]{5,4,3,2,1,0:T(8,128)(2,1)} %bitcast.125, bf16[2,4,4,4,24,384]{5,4,3,2,1,0:T(8,128)(2,1)} %bitcast.126, bf16[2,4,4,4,24,512]{5,4,3,2,1,0:T(8,128)(2,1)} %bitcast.122), custom_call_target="tpu_custom_call" | custom-call | tf_op jit(solution)/shard_map/reduce_gradients/pallas_call | solution.py:340
  240.6 1.4 copy.36
  242.0 1.5 copy.47
  243.5 1.4 copy.48
  (87 shorter events, 4.7 us)
Async XLA Ops:
  0.6 126.1 %copy-start = (bf16[768,2048]{1,0:T(8,128)(2,1)S(1)}, bf16[768,2048]{1,0:T(8,128)(2,1)}, u32[]{:S(2)}) copy-start(bf16[768,2048]{1,0:T(8,128)(2,1)} %param.15) | copy-start | bytes 9437188
  67.5 9.4 %copy-start.9 = (bf16[32,16,768]{2,1,0:T(8,128)(2,1)S(1)}, bf16[32,16,768]{2,1,0:T(8,128)(2,1)}, u32[]{:S(2)}) copy-start(bf16[32,16,768]{2,1,0:T(8,128)(2,1)} %gather_fusion) | copy-start | bytes 2359300
  70.0 0.9 copy-start.4
  71.7 17.0 %collective-permute-start = (bf16[256,768]{1,0:T(8,128)(2,1)S(1)}, bf16[256,768]{1,0:T(8,128)(2,1)}, u32[]{:S(2)}, u32[]{:S(2)}) collective-permute-start(bf16[256,768]{1,0:T(8,128)(2,1)S(1)} %get-tuple-element.26), channel_id=1, source_target_pairs={{0,1},{1,2},{2,3},{3,4},{4,5},{5,6},{6,7},{7,8},{8,9},{9,10},{10,1... | collective-permute-start | bytes 1179656 | tf_op jit(solution)/shard_map/ppermute | solution.py:383
  75.6 11.2 %collective-permute-start.1 = (bf16[256,768]{1,0:T(8,128)(2,1)}, bf16[256,768]{1,0:T(8,128)(2,1)}, u32[]{:S(2)}, u32[]{:S(2)}) collective-permute-start(bf16[256,768]{1,0:T(8,128)(2,1)} %get-tuple-element.27), channel_id=1, source_target_pairs={{1,0},{2,1},{3,2},{4,3},{5,4},{6,5},{7,6},{8,7},{9,8},{10,9},{11,1... | collective-permute-start | bytes 1179656 | tf_op jit(solution)/shard_map/ppermute | solution.py:384
  79.9 8.7 %copy-start.5 = (bf16[512,768]{1,0:T(8,128)(2,1)S(1)}, bf16[512,768]{1,0:T(8,128)(2,1)}, u32[]{:S(2)}) copy-start(bf16[512,768]{1,0:T(8,128)(2,1)} %copy-done.4) | copy-start | bytes 2359300
  79.9 8.7 %copy-start.13 = (f32[512,384]{0,1:T(8,128)S(1)}, f32[512,384]{0,1:T(8,128)}, u32[]{:S(2)}) copy-start(f32[512,384]{0,1:T(8,128)} %fusion.56) | copy-start | bytes 2359300
  103.8 13.2 %collective-permute-start.2 = (bf16[128,768]{1,0:T(8,128)(2,1)S(1)}, bf16[128,768]{1,0:T(8,128)(2,1)S(1)}, u32[]{:S(2)}, u32[]{:S(2)}) collective-permute-start(bf16[128,768]{1,0:T(8,128)(2,1)S(1)} %get-tuple-element.28), channel_id=1, source_target_pairs={{0,1},{1,2},{2,3},{3,4},{4,5},{5,6},{6,7},{7,8},{8,9},{9,10},{10,1... | collective-permute-start | bytes 589832 | tf_op jit(solution)/shard_map/ppermute | solution.py:383
  108.5 6.4 %collective-permute-start.3 = (bf16[128,768]{1,0:T(8,128)(2,1)S(1)}, bf16[128,768]{1,0:T(8,128)(2,1)S(1)}, u32[]{:S(2)}, u32[]{:S(2)}) collective-permute-start(bf16[128,768]{1,0:T(8,128)(2,1)S(1)} %get-tuple-element.29), channel_id=1, source_target_pairs={{1,0},{2,1},{3,2},{4,3},{5,4},{6,5},{7,6},{8,7},{9,8},{10,9},{11,1... | collective-permute-start | bytes 589832 | tf_op jit(solution)/shard_map/ppermute | solution.py:384
  114.9 0.7 copy-start.31
  117.0 3.1 %copy-start.2 = (f32[256,768]{1,0:T(8,128)S(1)}, f32[256,768]{1,0:T(8,128)}, u32[]{:S(2)}) copy-start(f32[256,768]{1,0:T(8,128)} %reduce_sum.31) | copy-start | bytes 2359300
  117.1 3.1 %copy-start.25 = (bf16[2,384,768]{2,1,0:T(8,128)(2,1)S(1)}, bf16[2,384,768]{2,1,0:T(8,128)(2,1)}, u32[]{:S(2)}) copy-start(bf16[2,384,768]{2,1,0:T(8,128)(2,1)} %param.14) | copy-start | bytes 3538948
  117.1 2.4 copy-start.28
  119.4 0.7 copy-start.18
  129.3 1.2 copy-start.16
  130.5 1.3 copy-start.26
  130.6 1.5 copy-start.30
  130.9 0.9 copy-start.21
  132.5 4.3 %copy-start.7 = (bf16[256,384]{1,0:T(8,128)(2,1)}, bf16[256,384]{1,0:T(8,128)(2,1)S(1)}, u32[]{:S(2)}) copy-start(bf16[256,384]{1,0:T(8,128)(2,1)S(1)} %fusion.23) | copy-start | bytes 589828
  132.5 4.3 %copy-start.17 = (bf16[128,2048]{1,0:T(8,128)(2,1)S(1)}, bf16[128,2048]{1,0:T(8,128)(2,1)}, u32[]{:S(2)}) copy-start(bf16[128,2048]{1,0:T(8,128)(2,1)} %copy-done.16) | copy-start | bytes 1572868
  132.5 4.3 %copy-start.24 = (f32[128,768]{1,0:T(8,128)S(1)}, f32[128,768]{1,0:T(8,128)}, u32[]{:S(2)}) copy-start(f32[128,768]{1,0:T(8,128)} %reduce_sum.32) | copy-start | bytes 1179652
  136.8 2.6 %copy-start.19 = (bf16[256,384]{1,0:T(8,128)(2,1)S(1)}, bf16[256,384]{1,0:T(8,128)(2,1)}, u32[]{:S(2)}) copy-start(bf16[256,384]{1,0:T(8,128)(2,1)} %copy-done.18) | copy-start | bytes 589828
  140.3 19.8 %collective-permute-start.4 = (bf16[128,384]{1,0:T(8,128)(2,1)}, bf16[128,384]{1,0:T(8,128)(2,1)}, u32[]{:S(2)}, u32[]{:S(2)}) collective-permute-start(bf16[128,384]{1,0:T(8,128)(2,1)} %get-tuple-element.30), channel_id=1, source_target_pairs={{1,0},{2,1},{3,2},{4,3},{5,4},{6,5},{7,6},{8,7},{9,8},{10,9},{11,1... | collective-permute-start | bytes 294920 | tf_op jit(solution)/shard_map/ppermute | solution.py:384
  141.6 17.0 %collective-permute-start.5 = (bf16[128,384]{1,0:T(8,128)(2,1)}, bf16[128,384]{1,0:T(8,128)(2,1)}, u32[]{:S(2)}, u32[]{:S(2)}) collective-permute-start(bf16[128,384]{1,0:T(8,128)(2,1)} %get-tuple-element.31), channel_id=1, source_target_pairs={{0,1},{1,2},{2,3},{3,4},{4,5},{5,6},{6,7},{7,8},{8,9},{9,10},{10,1... | collective-permute-start | bytes 294920 | tf_op jit(solution)/shard_map/ppermute | solution.py:383
  152.9 2.4 copy-start.8
  152.9 2.4 copy-start.29
  153.0 2.8 %copy-start.32 = (bf16[128,768]{1,0:T(8,128)(2,1)S(1)}, bf16[128,768]{1,0:T(8,128)(2,1)}, u32[]{:S(2)}) copy-start(bf16[128,768]{1,0:T(8,128)(2,1)} %copy-done.31) | copy-start | bytes 589828
  155.4 1.1 copy-start.14
  156.4 1.0 copy-start.23
  156.4 1.1 copy-start.27
  157.5 2.7 %copy-start.3 = (f32[256,768]{1,0:T(8,128)S(1)}, f32[256,768]{1,0:T(8,128)}, u32[]{:S(2)}) copy-start(f32[256,768]{1,0:T(8,128)} %reduce_sum.31) | copy-start | bytes 2359300
  157.5 2.7 %copy-start.11 = (f32[256,768]{1,0:T(8,128)S(1)}, f32[256,768]{1,0:T(8,128)}, u32[]{:S(2)}) copy-start(f32[256,768]{1,0:T(8,128)} %fusion.46) | copy-start | bytes 2359300
  157.5 2.7 %copy-start.22 = (bf16[256,768]{1,0:T(8,128)(2,1)S(1)}, bf16[256,768]{1,0:T(8,128)(2,1)}, u32[]{:S(2)}) copy-start(bf16[256,768]{1,0:T(8,128)(2,1)} %copy-done.21) | copy-start | bytes 1179652
  165.7 2.3 copy-start.6
  173.6 1.1 copy-start.12
  173.6 1.3 copy-start.20
  174.9 1.1 copy-start.15
  183.2 1.8 copy-start.10
  187.0 57.9 %copy-start.1 = (bf16[768,2048]{1,0:T(8,128)(2,1)S(1)}, bf16[768,2048]{1,0:T(8,128)(2,1)}, u32[]{:S(2)}) copy-start(bf16[768,2048]{1,0:T(8,128)(2,1)} %param.15) | copy-start | bytes 9437188

commit v2 on v1

--- a/solution.py
+++ b/solution.py
@@ -7,8 +7,6 @@
 from jax.experimental.pallas import tpu as pltpu
 from jax.sharding import PartitionSpec as P
 
-SPREAD_FINE = 256
-SPREAD_COARSE = 128
 MESH = pl.DeviceIdType.MESH
 CHUNK = 512
 ORDERS = ((0, 1, 2), (1, 2, 0), (2, 0, 1))
@@ -271,45 +269,345 @@
         return f32(self.acc3[here]) + f32(self.last[0]) + f32(self.last[1]) + f32(self.last[2])
 
 
-N_REDUCE = 3 * (1 + 6 + 6 + 3) + 3
-
-
-def reduce_kernel(terms0, terms1, terms2, kernel_out, mixer_out, readout_out, *scratch):
-    parts_scratch, (joined, send_sems, recv_sems) = scratch[:-3], scratch[-3:]
+def part_scratch(width):
+    unit = (24, width)
+    return [
+        pltpu.VMEM(shape + unit, jnp.bfloat16)
+        for shape in ((4, 4, 4), (4, 4, 4), (8, 2, 4), (4, 4), (8, 2), (4,), (3,))
+    ]
+
+
+def gelu(values):
+    return 0.5 * values * (1.0 + lax.erf(values * (1.0 / math.sqrt(2.0))))
+
+
+def gelu_slope(values):
+    cumulative = 0.5 * (1.0 + lax.erf(values * (1.0 / math.sqrt(2.0))))
+    density = jnp.exp(-0.5 * values * values) * (1.0 / math.sqrt(2.0 * math.pi))
+    return cumulative + values * density
+
+
+def bf(values):
+    return values.astype(jnp.bfloat16)
+
+
+def dot(left, right):
+    return jnp.dot(left, right, preferred_element_type=jnp.float32)
+
+
+def dot_nt(left, right):
+    return lax.dot_general(
+        left, right, (((1,), (1,)), ((), ())), preferred_element_type=jnp.float32
+    )
+
+
+def flat(values):
+    return values.reshape(-1, values.shape[-1])
+
+
+def row_blocks(count, step, body):
+    @pl.loop(0, count // step)
+    def _(at):
+        body(pl.multiple_of(at * step, step))
+
+
+STEP = 16
+HALF = 64
+INNER = 384
+CH = 768
+
+
+def conv_forward(act, kernel, inner, edge_out, edge_in, send, after, before, seq, groups):
+    low, high = flat(act[:, 0:HALF, :]), flat(act[:, HALF:128, :])
+    shape = (act.shape[0], HALF, INNER)
+    edge_out[0] = bf(dot(high, kernel[0])).reshape(shape)
+    from_before = send(edge_out.at[0], edge_in.at[0], after)
+    edge_out[1] = bf(dot(low, kernel[2])).reshape(shape)
+    from_after = send(edge_out.at[1], edge_in.at[1], before)
+    inner[:, 0:HALF, :] = (dot(low, kernel[1]) + dot(high, kernel[2])).reshape(shape)
+    inner[:, HALF:128, :] = (dot(high, kernel[1]) + dot(low, kernel[0])).reshape(shape)
+    return from_before, from_after
+
+
+def finish_inner(inner, gated, edge_in, copies, seq, groups):
+    copies[0].wait_recv()
+    copies[1].wait_recv()
+    keeps = (jnp.where(seq == 0, 0.0, 1.0), jnp.where(seq == groups - 1, 0.0, 1.0))
+    for side in range(2):
+
+        @pl.loop(0, inner.shape[0])
+        def _(group):
+            for row in range(0, HALF, STEP):
+                rows = slice(side * HALF + row, side * HALF + row + STEP)
+                total = inner[group, rows, :] + f32(edge_in[side, group, row : row + STEP, :]) * keeps[side]
+                inner[group, rows, :] = total
+                gated[group, rows, :] = bf(gelu(total))
+
+
+def exchange_grads(wide, send, after, before):
+    from_after = send(wide.at[1, :, pl.ds(0, HALF)], wide.at[0, :, pl.ds(HALF, HALF)], before)
+    from_before = send(wide.at[1, :, pl.ds(HALF, HALF)], wide.at[2, :, pl.ds(0, HALF)], after)
+    wide[0, :, 0:HALF, :] = wide[1, :, HALF:128, :]
+    wide[2, :, HALF:128, :] = wide[1, :, 0:HALF, :]
+    return from_after, from_before
+
+
+def finish_exchange(wide, copies, seq, groups):
+    copies[0].wait_recv()
+    copies[1].wait_recv()
+    zeros = jnp.zeros((wide.shape[1], HALF, INNER), jnp.bfloat16)
+
+    @pl.when(seq == groups - 1)
+    def _():
+        wide[0, :, HALF:128, :] = zeros
+
+    @pl.when(seq == 0)
+    def _():
+        wide[2, :, 0:HALF, :] = zeros
+
+
+def gradient_rows(transposed, right, store):
+    @pl.loop(0, 4)
+    def _(y):
+        result = dot(transposed[pl.ds(pl.multiple_of(y * 192, 64), 192), :], right())
+        for x_hi in range(2):
+            for z in range(4):
+                row = 24 * (4 * x_hi + z)
+                store(y, x_hi, z, bf(result[row : row + 24]))
+
+
+def blocks_kernel(
+    landed, lane_position, length_ref, targets, kernels, mixers, readout,
+    kernel_out, mixer_out, readout_out, trunk_out,
+    kernels_v, mixers_v, readout_v, targets_v, local_sems,
+    hid, act1, inner1, gated1, mixed, first, act2, inner2, gated2, second, logits, logit_grad,
+    upper, woven, wide2, wide1, lower, act1_t, act2_t, second_t, mixer_left, mixer_right,
+    edge1_out, edge1_in, edge2_out, edge2_in, terms0, terms1, terms2, *rest
+):
+    parts_scratch, (joined, send_sems, recv_sems) = rest[:-3], rest[-3:]
     coords, core = place()
-    dp = lax.axis_index("dp")
+    dp, seq = lax.axis_index("dp"), lax.axis_index("seq")
+    groups = lax.axis_size("seq")
+    loads = []
+    for at, (src, dst) in enumerate(
+        (
+            (kernels.at[0], kernels_v.at[0]),
+            (mixers, mixers_v),
+            (kernels.at[1], kernels_v.at[1]),
+            (readout, readout_v),
+            (targets, targets_v),
+        )
+    ):
+        loads.append(pltpu.make_async_copy(src, dst, local_sems.at[at]))
+        loads[-1].start()
+    after, before = (dp, lax.rem(seq + 1, groups)), (dp, lax.rem(seq + groups - 1, groups))
     send = Sender(send_sems, recv_sems)
+    all_terms = (terms0, terms1, terms2)
     parts = [
-        Part(ORDERS[at], terms, parts_scratch[7 * at : 7 * at + 7], send, coords, core)
-        for at, terms in enumerate((terms0, terms1, terms2))
+        Part(ORDERS[at], all_terms[at], parts_scratch[7 * at : 7 * at + 7], send, coords, core)
+        for at in range(3)
     ]
     pair_x = (coords[0] + 1 - 2 * lax.rem(coords[0], 2),) + coords[1:]
     partner = device_at(coords, 1 - core)
     group = [partner, device_at(pair_x, core), device_at(pair_x, 1 - core)]
     greet(
         [device_at(moved(coords, axis, k), core) for axis in range(3) for k in (1, 2, 3)]
-        + [partner, device_at(pair_x, 1 - core)]
+        + [partner, device_at(pair_x, 1 - core), after, before]
     )
-    for part in parts:
-        part.start_pair()
-    for part in parts:
-        part.end_pair()
-        part.start_level(0)
-    for part in parts:
-        part.relay_level(0)
-    for part in parts:
-        part.end_level(0)
-        part.start_level(1)
-    for part in parts:
-        part.relay_level(1)
-    for part in parts:
-        part.end_level(1)
-        part.start_last()
+    length = length_ref[0]
+
+    blocks = flat(landed[...])
+    for group_at in range(4):
+        spot = 4 * lax.broadcasted_iota(jnp.int32, (128, 512), 0) + group_at
+        chosen = (lane_position[...] == spot) & (spot + seq * 512 < length)
+        hid[group_at] = bf(dot(jnp.where(chosen, 1.0, 0.0).astype(jnp.bfloat16), blocks))
+
+    for group_at in range(4):
+
+        def gelu_rows(row, group_at=group_at):
+            act1[group_at, pl.ds(row, STEP), :] = bf(gelu(f32(hid[group_at, pl.ds(row, STEP), :])))
+
+        row_blocks(128, STEP, gelu_rows)
+
+    loads[0].wait()
+    edges = conv_forward(act1, kernels_v.at[0], inner1, edge1_out, edge1_in, send, after, before, seq, groups)
+    act1_t[...] = flat(act1[...]).T
+    finish_inner(inner1, gated1, edge1_in, edges, seq, groups)
+    loads[1].wait()
+    mixed[...] = dot(flat(gated1[...]), mixers_v[0]).reshape(mixed.shape)
+    for pair in range(2):
+
+        def pool_rows(row, pair=pair):
+            rows = pl.ds(row, STEP)
+            total = (f32(hid[2 * pair, rows, :]) + mixed[2 * pair, rows, :]) + (
+                f32(hid[2 * pair + 1, rows, :]) + mixed[2 * pair + 1, rows, :]
+            )
+            pooled = bf(total * 0.5)
+            first[pair, rows, :] = pooled
+            act2[pair, rows, :] = bf(gelu(f32(pooled)))
+
+        row_blocks(128, STEP, pool_rows)
+
+    loads[2].wait()
+    edges = conv_forward(act2, kernels_v.at[1], inner2, edge2_out, edge2_in, send, after, before, seq, groups)
+    act2_t[...] = flat(act2[...]).T
+    finish_inner(inner2, gated2, edge2_in, edges, seq, groups)
+    mixed[0:2] = dot(flat(gated2[...]), mixers_v[1]).reshape(2, 128, CH)
+
+    def pool_again(row):
+        rows = pl.ds(row, STEP)
+        total = (f32(first[0, rows, :]) + mixed[0, rows, :]) + (f32(first[1, rows, :]) + mixed[1, rows, :])
+        second[rows, :] = bf(total * 0.5)
+
+    row_blocks(128, STEP, pool_again)
+    loads[3].wait()
+    loads[4].wait()
+    logits[...] = dot(second[...], readout_v[...])
+    loss_scale = 2.0 / math.sqrt(lax.axis_size("dp") * groups * 128)
+
+    def loss_rows(row):
+        rows = pl.ds(row, 8)
+        values = logits[rows, :]
+        small = jnp.exp(-jnp.abs(values))
+        softplus = jnp.maximum(values, 0.0) + jnp.log1p(small)
+        sigmoid = jnp.where(values >= 0.0, 1.0, small) / (1.0 + small)
+        bins = seq * 128 + row + lax.broadcasted_iota(jnp.int32, (8, 1), 0)
+        valid = jnp.where(bins * 4 < length, loss_scale, 0.0)
+        mixed_rows = valid * (softplus - targets_v[rows, :].astype(jnp.float32)) * sigmoid
+        logits[rows, :] = mixed_rows
+
+    row_blocks(128, 8, loss_rows)
+    logit_grad[...] = bf(logits[...])
+    second_t[...] = second[...].T
+    for index in range(4):
+        x_lo, half = index // 2, index % 2
+
+        def store(y, x_hi, z, block, x_lo=x_lo, half=half):
+            terms2[half, z, 2 * x_hi + x_lo, y] = block
+
+        gradient_rows(second_t, lambda i=index: logit_grad[:, 512 * i : 512 * i + 512], store)
+    parts[2].start_pair()
+
+    upper[...] = bf(dot_nt(logit_grad[...], readout_v[...]) * 0.5)
+    back = dot_nt(upper[...], mixers_v[1])
+    logits[:, 0:INNER] = back
+
+    def coarse_rows(row):
+        rows = pl.ds(row, STEP)
+        back_rows = logits[rows, 0:INNER]
+        for pair in range(2):
+            wide2[1, pair, rows, :] = bf(back_rows * gelu_slope(inner2[pair, rows, :]))
+
+    row_blocks(128, STEP, coarse_rows)
+    edges = exchange_grads(wide2, send, after, before)
+    parts[2].end_pair()
+    parts[2].start_level(0)
+
+    def store_coarse(y, x_hi, z, block):
+        terms1[0, y, z, 2 * x_hi] = block
+
+    gradient_rows(act2_t, lambda: flat(wide2[1]), store_coarse)
+    finish_exchange(wide2, edges, seq, groups)
+    mixed[0:2] = (
+        dot_nt(flat(wide2[0]), kernels_v[1, 0])
+        + dot_nt(flat(wide2[1]), kernels_v[1, 1])
+        + dot_nt(flat(wide2[2]), kernels_v[1, 2])
+    ).reshape(2, 128, CH)
+    trunk_scale = math.sqrt(lax.axis_size("dp") * groups * 128) * 0.5
+
+    def trunk_rows(row):
+        rows = pl.ds(row, STEP)
+        upper_rows = f32(upper[rows, :])
+        for pair in range(2):
+            grad = upper_rows + mixed[pair, rows, :] * gelu_slope(f32(first[pair, rows, :]))
+            scaled = grad * trunk_scale
+            for at in range(6):
+                woven[at, pl.ds(2 * row + pair, STEP, stride=2), :] = scaled[:, 128 * at : 128 * at + 128]
+            lower[pair, rows, :] = bf(grad * 0.5)
+
+    row_blocks(128, STEP, trunk_rows)
+    for at in range(6):
+        trunk_out[:, 128 * at : 128 * at + 128] = woven[at]
+    parts[2].relay_level(0)
+    back = dot_nt(flat(lower[...]), mixers_v[0])
+    mixed[0:2, :, 0:INNER] = back.reshape(2, 128, INNER)
+    for pair in range(2):
+
+        def fine_rows(row, pair=pair):
+            rows = pl.ds(row, STEP)
+            back_rows = mixed[pair, rows, 0:INNER]
+            for side in range(2):
+                wide1[1, 2 * pair + side, rows, :] = bf(back_rows * gelu_slope(inner1[2 * pair + side, rows, :]))
+
+        row_blocks(128, STEP, fine_rows)
+
+    edges = exchange_grads(wide1, send, after, before)
+    parts[2].end_level(0)
+    parts[2].start_level(1)
+
+    def store_third(y, x_hi, z, block):
+        terms0[1, 2 * x_hi + 1, y, z] = block
+
+    def store_fifth(y, x_hi, z, block):
+        terms1[1, y, z, 2 * x_hi] = block
+
+    gradient_rows(act2_t, lambda: flat(wide2[0]), store_third)
+    gradient_rows(act2_t, lambda: flat(wide2[2]), store_fifth)
+
+    column = lax.broadcasted_iota(jnp.int32, (CH, INNER), 1)
+    target_row = column + 12 * lax.shift_right_logical(column * 43691, 19)
+    row_at = lax.broadcasted_iota(jnp.int32, (CH, INNER), 0)
+    picks = jnp.where(row_at == target_row, 1.0, 0.0).astype(jnp.bfloat16)
+    mixer_left[:, 0:512] = bf(dot_nt(picks, flat(gated1[...])))
+    picks = jnp.where(row_at == target_row + 12, 1.0, 0.0).astype(jnp.bfloat16)
+    mixer_left[:, 512:768] = bf(dot_nt(picks, flat(gated2[...])))
+    for at in range(4):
+        mixer_right[128 * at : 128 * at + 128] = lower[at // 2]
+    for at in range(4, 6):
+        mixer_right[128 * at : 128 * at + 128] = upper[...]
+    for half in range(2):
+
+        def store_mixer(y, x_hi, z, block, half=half):
+            terms1[half, y, z, 2 * x_hi + 1] = block
+
+        gradient_rows(mixer_left, lambda h=half: mixer_right[:, INNER * h : INNER * h + INNER], store_mixer)
+    parts[1].start_pair()
+
+    def fine_store(tap):
+        def store(y, x_hi, z, block):
+            terms0[tap % 2, 2 * x_hi + tap // 2, y, z] = block
+
+        return store
+
+    gradient_rows(act1_t, lambda: flat(wide1[1]), fine_store(1))
+    finish_exchange(wide1, edges, seq, groups)
+    parts[2].relay_level(1)
+    gradient_rows(act1_t, lambda: flat(wide1[0]), fine_store(0))
+    parts[1].end_pair()
+    parts[1].start_level(0)
+    gradient_rows(act1_t, lambda: flat(wide1[2]), fine_store(2))
+    parts[0].start_pair()
+    parts[2].end_level(1)
+    parts[2].start_last()
+    parts[1].relay_level(0)
+    parts[0].end_pair()
+    parts[0].start_level(0)
+    readout_out[...] = parts[2].end_last()
+    parts[1].end_level(0)
+    parts[1].start_level(1)
+    parts[0].relay_level(0)
+    parts[1].relay_level(1)
+    parts[0].end_level(0)
+    parts[0].start_level(1)
+    parts[1].end_level(1)
+    parts[1].start_last()
+    parts[0].relay_level(1)
+    joined[dp, :, 384:768] = parts[1].end_last()
+    parts[0].end_level(1)
+    parts[0].start_last()
     joined[dp, :, 0:384] = parts[0].end_last()
-    joined[dp, :, 384:768] = parts[1].end_last()
     mine = joined.at[dp]
     last = [send(mine, mine, device) for device in group]
-    readout_out[...] = parts[2].end_last()
     for copy in last:
         copy.wait_recv()
     for index in range(4):
@@ -327,190 +625,79 @@
     send.finish()
 
 
-def part_scratch(width):
-    unit = (24, width)
-    return [
-        pltpu.VMEM(shape + unit, jnp.bfloat16)
-        for shape in ((4, 4, 4), (4, 4, 4), (8, 2, 4), (4, 4), (8, 2), (4,), (3,))
-    ]
-
-
-def reduce_terms(terms):
-    vmem = pl.BlockSpec(memory_space=pltpu.VMEM)
+N_REDUCE = 3 * (1 + 6 + 6 + 3) + 3 + 8
+
+
+def blocks_and_gradients(landed, lane_position, length, targets, kernels, mixers, readout):
+    vmem, anywhere = pl.BlockSpec(memory_space=pltpu.VMEM), pl.BlockSpec(memory_space=pl.ANY)
+    bf16, single = jnp.bfloat16, jnp.float32
     return pl.pallas_call(
-        reduce_kernel,
+        blocks_kernel,
         out_shape=(
-            jax.ShapeDtypeStruct((6, 24, 96), jnp.float32),
-            jax.ShapeDtypeStruct((2, 12, 192), jnp.float32),
-            jax.ShapeDtypeStruct((24, 512), jnp.float32),
+            jax.ShapeDtypeStruct((6, 24, 96), single),
+            jax.ShapeDtypeStruct((2, 12, 192), single),
+            jax.ShapeDtypeStruct((24, 512), single),
+            jax.ShapeDtypeStruct((256, CH), single),
         ),
-        in_specs=[vmem] * 3,
-        out_specs=[vmem] * 3,
-        scratch_shapes=[s for width in WIDTHS for s in part_scratch(width)]
+        in_specs=[vmem, vmem, pl.BlockSpec(memory_space=pltpu.SMEM)] + [anywhere] * 4,
+        out_specs=[vmem] * 4,
+        scratch_shapes=[
+            pltpu.VMEM((2, 3, CH, INNER), bf16),
+            pltpu.VMEM((2, INNER, CH), bf16),
+            pltpu.VMEM((CH, 2048), bf16),
+            pltpu.VMEM((128, 2048), jnp.int32),
+            pltpu.SemaphoreType.DMA((5,)),
+            pltpu.VMEM((4, 128, CH), bf16),
+            pltpu.VMEM((4, 128, CH), bf16),
+            pltpu.VMEM((4, 128, INNER), single),
+            pltpu.VMEM((4, 128, INNER), bf16),
+            pltpu.VMEM((4, 128, CH), single),
+            pltpu.VMEM((2, 128, CH), bf16),
+            pltpu.VMEM((2, 128, CH), bf16),
+            pltpu.VMEM((2, 128, INNER), single),
+            pltpu.VMEM((2, 128, INNER), bf16),
+            pltpu.VMEM((128, CH), bf16),
+            pltpu.VMEM((128, 2048), single),
+            pltpu.VMEM((128, 2048), bf16),
+            pltpu.VMEM((128, CH), bf16),
+            pltpu.VMEM((6, 256, 128), single),
+            pltpu.VMEM((3, 2, 128, INNER), bf16),
+            pltpu.VMEM((3, 4, 128, INNER), bf16),
+            pltpu.VMEM((2, 128, CH), bf16),
+            pltpu.VMEM((CH, 512), bf16),
+            pltpu.VMEM((CH, 256), bf16),
+            pltpu.VMEM((CH, 128), bf16),
+            pltpu.VMEM((CH, CH), bf16),
+            pltpu.VMEM((CH, CH), bf16),
+            pltpu.VMEM((2, 4, HALF, INNER), bf16),
+            pltpu.VMEM((2, 4, HALF, INNER), bf16),
+            pltpu.VMEM((2, 2, HALF, INNER), bf16),
+            pltpu.VMEM((2, 2, HALF, INNER), bf16),
+        ]
+        + [pltpu.VMEM((2, 4, 4, 4, 24, width), bf16) for width in WIDTHS]
+        + [s for width in WIDTHS for s in part_scratch(width)]
         + [
-            pltpu.VMEM((4, 24, 768), jnp.float32),
+            pltpu.VMEM((4, 24, CH), single),
             pltpu.SemaphoreType.DMA((N_REDUCE,)),
             pltpu.SemaphoreType.DMA((N_REDUCE,)),
         ],
         compiler_params=pltpu.CompilerParams(
-            collective_id=2, has_side_effects=True, vmem_limit_bytes=56 << 20
+            collective_id=2, has_side_effects=True, vmem_limit_bytes=60 << 20
         ),
-        name="reduce_gradients",
-    )(*terms)
-
-
-def arrange_terms(kernel_terms, mixer_terms, readout_terms):
-    bf16 = jnp.bfloat16
-    kernels = kernel_terms.astype(bf16).reshape(6, 768, 384)
-    mixers = mixer_terms.astype(bf16).reshape(2, 32, 12, 768).transpose(1, 0, 2, 3).reshape(768, 2, 384)
-    first = kernels[:4].reshape(2, 2, 4, 2, 4, 24, 384)
-    second = jnp.concatenate([kernels[4:], mixers.transpose(1, 0, 2)]).reshape(2, 2, 4, 2, 4, 24, 384)
-    third = readout_terms.astype(bf16).reshape(4, 2, 4, 24, 2, 2, 512).transpose(4, 5, 0, 1, 2, 3, 6)
-    return (
-        first.transpose(1, 3, 0, 2, 4, 5, 6).reshape(2, 4, 4, 4, 24, 384),
-        second.transpose(1, 2, 4, 3, 0, 5, 6).reshape(2, 4, 4, 4, 24, 384),
-        third.transpose(1, 4, 3, 0, 2, 5, 6).reshape(2, 4, 4, 4, 24, 512),
-    )
-
-
-def with_halo(shard, sides, width):
-    for axis, dim in sides:
-        size, length = (lax.axis_size(axis), shard.shape[dim])
-        up = [(i, (i + 1) % size) for i in range(size - 1)]
-        down = [(j, i) for i, j in up]
-        last = lax.slice_in_dim(shard, length - width, length, axis=dim)
-        leading = lax.slice_in_dim(shard, 0, width, axis=dim)
-        before = lax.ppermute(last, axis, up)
-        after = lax.ppermute(leading, axis, down)
-        shard = jnp.concatenate([before, shard, after], axis=dim)
-    return shard
-
-
-def gelu_exact(values):
-    return 0.5 * values * (1.0 + lax.erf(values * (1.0 / math.sqrt(2.0))))
-
-
-def gelu_slope(values):
-    cumulative = 0.5 * (1.0 + lax.erf(values * (1.0 / math.sqrt(2.0))))
-    density = jnp.exp(-0.5 * values * values) * (1.0 / math.sqrt(2.0 * math.pi))
-    return cumulative + values * density
-
-
-def matmul(left_side, right_side):
-    return jnp.dot(left_side, right_side, preferred_element_type=jnp.float32)
-
-
-def times_transposed(left_side, right_side):
-    return lax.dot_general(
-        left_side, right_side, (((1,), (1,)), ((), ())), preferred_element_type=jnp.float32
-    )
-
-
-def transposed_times(left_side, right_side):
-    return lax.dot_general(
-        left_side, right_side, (((0,), (0,)), ((), ())), preferred_element_type=jnp.float32
-    )
-
-
-def spread_taps(extended, spread, row_count):
-    return (
-        extended[0:row_count],
-        extended[spread : spread + row_count],
-        extended[2 * spread : 2 * spread + row_count],
-    )
-
-
-def block_rest(hidden, shifted, kernel, mixing):
-    inner_sum = (
-        matmul(shifted[0], kernel[0])
-        + matmul(shifted[1], kernel[1])
-        + matmul(shifted[2], kernel[2])
-    )
-    gated_out = gelu_exact(inner_sum).astype(jnp.bfloat16)
-    output = hidden.astype(jnp.float32) + matmul(gated_out, mixing)
-    pooled = (output.reshape(-1, 2, output.shape[1]).sum(axis=1) * 0.5).astype(jnp.bfloat16)
-    return (pooled, inner_sum, gated_out)
-
-
-def block_backward(upstream, shifted, inner_sum, gated_out, mixing):
-    mixing_grad = transposed_times(gated_out, upstream)
-    inner_grad = (times_transposed(upstream, mixing) * gelu_slope(inner_sum)).astype(jnp.bfloat16)
-    kernel_grad = jnp.stack(
-        [transposed_times(shifted[tap_index], inner_grad) for tap_index in range(3)]
-    )
-    return (kernel_grad, mixing_grad, inner_grad)
+        name="blocks",
+    )(landed, lane_position, length, targets, kernels, mixers, readout)
 
 
 def shards(embeddings, layout, lengths, targets, projection, kernels, mixers, readout):
-    groups = lax.axis_size("seq")
-    windows_total = lax.axis_size("dp")
-    device = lax.axis_index("seq")
-    local_rows = embeddings[0, 0]
-    row_count = local_rows.shape[0]
-    block_rows = row_count // groups
-    channels = projection.shape[1]
-    layout_table = layout[0]
-    length = lengths[0]
-    shard_ids = jnp.arange(groups, dtype=jnp.int32)
-    own_column = lax.dynamic_index_in_dim(layout_table, device, axis=1, keepdims=False)
-    matches = (own_column[:, None] == shard_ids[None, :]).astype(jnp.int32)
-    source_index = jnp.sum(shard_ids[:, None] * matches, axis=0)
-    received = project_and_exchange(local_rows, projection)
-    hidden = jnp.take(received, source_index, axis=0).reshape(row_count, channels)
-    positions = device * row_count + jnp.arange(row_count, dtype=jnp.int32)
-    hidden = jnp.where((positions < length)[:, None], hidden, jnp.zeros_like(hidden))
-    fine_spread = SPREAD_FINE
-    coarse_spread = SPREAD_COARSE
-    half_count = row_count // 2
-    fine_active = gelu_exact(hidden.astype(jnp.float32)).astype(jnp.bfloat16)
-    fine_wide = with_halo(fine_active, (("seq", 0),), fine_spread)
-    fine_shifted = spread_taps(fine_wide, fine_spread, row_count)
-    first_pooled, fine_inner, fine_gated = block_rest(hidden, fine_shifted, kernels[0], mixers[0])
-    coarse_active = gelu_exact(first_pooled.astype(jnp.float32)).astype(jnp.bfloat16)
-    coarse_wide = with_halo(coarse_active, (("seq", 0),), coarse_spread)
-    coarse_shifted = spread_taps(coarse_wide, coarse_spread, half_count)
-    second, coarse_inner, coarse_gated = block_rest(
-        first_pooled, coarse_shifted, kernels[1], mixers[1]
-    )
-    bin_count = row_count // 4
-    logits = matmul(second, readout)
-    bin_ids = device * bin_count + jnp.arange(bin_count, dtype=jnp.int32)
-    valid_bins = (bin_ids * 4 < length).astype(jnp.float32)
-    loss_scale = 2.0 / math.sqrt(windows_total * groups * bin_count)
-    target_values = targets[0].astype(jnp.float32)
-    logit_grad = (
-        loss_scale
-        * valid_bins[:, None]
-        * (jax.nn.softplus(logits) - target_values)
-        * jax.nn.sigmoid(logits)
-    ).astype(jnp.bfloat16)
-    readout_grad = transposed_times(second, logit_grad)
-    upper_grad = (times_transposed(logit_grad, readout) * 0.5).astype(jnp.bfloat16)
-    upper_rows = jnp.repeat(upper_grad, 2, axis=0)
-    coarse_kernel, coarse_mixing, coarse_grad = block_backward(
-        upper_rows, coarse_shifted, coarse_inner, coarse_gated, mixers[1]
-    )
-    grad_wide = with_halo(coarse_grad, (("seq", 0),), coarse_spread)
-    input_grad = (
-        times_transposed(
-            grad_wide[2 * coarse_spread : 2 * coarse_spread + half_count], kernels[1][0]
-        )
-        + times_transposed(coarse_grad, kernels[1][1])
-        + times_transposed(grad_wide[0:half_count], kernels[1][2])
-    )
-    first_grad = upper_rows.astype(jnp.float32) + input_grad * gelu_slope(
-        first_pooled.astype(jnp.float32)
-    )
-    trunk_grad = first_grad * (math.sqrt(windows_total * groups * bin_count) * 0.5)
-    lower_grad = (first_grad * 0.5).astype(jnp.bfloat16)
-    lower_rows = jnp.repeat(lower_grad, 2, axis=0)
-    fine_kernel, fine_mixing, fine_grad = block_backward(
-        lower_rows, fine_shifted, fine_inner, fine_gated, mixers[0]
-    )
-    kernel_terms = jnp.stack([fine_kernel, coarse_kernel])
-    mixer_terms = jnp.stack([fine_mixing, coarse_mixing])
-    kernel_total, mixer_total, readout_total = reduce_terms(
-        arrange_terms(kernel_terms, mixer_terms, readout_grad)
+    row_count = embeddings.shape[2]
+    block_rows = row_count // lax.axis_size("seq")
+    column = lax.dynamic_index_in_dim(layout[0], lax.axis_index("seq"), axis=1, keepdims=False)
+    lane_position = (
+        column[:, None] * block_rows + jnp.arange(block_rows, dtype=jnp.int32)[None, :]
+    ).reshape(1, row_count)
+    landed = project_and_exchange(embeddings[0, 0], projection)
+    kernel_total, mixer_total, readout_total, trunk_grad = blocks_and_gradients(
+        landed, lane_position, lengths, targets[0], kernels, mixers, readout
     )
     return (kernel_total.reshape(2, 3, 24, 96), mixer_total, readout_total, trunk_grad[None])
 

time: 246 us -> 167 us (0.68)
  Pallas kernels: 116 us -> 157 us
  matrix products: 39.8 us -> 0 us
  local copies, waits for them, and re-layouts: 45.3 us -> 7.06 us
  starting transfers between devices: 19.2 us -> 0 us
  other arithmetic: 12.7 us -> 0.97 us
  waiting for transfers between devices: 10.4 us -> 0 us
    pallas_call x1, Pallas kernels: 53.5 us -> 95.4 us  [blocks_and_gradients(): pl.pallas_call(blocks_kernel, out_shape=(jax.ShapeDtypeStruct((6, 24, 96)...]
    dot_general x24 -> x0, matrix products: 39.8 us -> none  [the longest x9 19.2 us: matmul(): return jnp.dot(left_side, right_side, preferred_element_type=jnp.float32)]
    reshape x10 -> x0, local copies, waits for them, and re-layouts: 21.5 us -> none  [the longest x2 7.17 us: arrange_terms(): readout_terms.astype(bf16).reshape(4, 2, 4, 24, 2, 2, 512)]
    ppermute x6 -> x0, starting transfers between devices: 19.2 us -> none  [the longest x3 15.1 us: with_halo(): before = lax.ppermute(last, axis, up)]
    ppermute x6 -> x0, waiting for transfers between devices: 10.4 us -> none  [the longest x3 10.4 us: with_halo(): after = lax.ppermute(leading, axis, down)]
    reduce_sum x3 -> x0, other arithmetic: 7.08 us -> none  [the longest x2 6.99 us: block_rest(): output.reshape(-1, 2, output.shape[1]).sum(axis=1) * 0.5]
    transpose x3 -> x0, local copies, waits for them, and re-layouts: 5.31 us -> none  [the longest x1 1.82 us: arrange_terms(): mixer_terms.astype(bf16).reshape(2, 32, 12, 768).transpose(1, 0, 2, 3)]
    convert_element_type x3 -> x0, other arithmetic: 4.33 us -> none  [the longest x2 3.03 us: shards(): fine_active = gelu_exact(hidden.astype(jnp.float32)).astype(jnp.bfloat16)]
  transfers between devices with their start and end apart: 6 -> 0, of which waited for: 2 -> 0; matrix products, arithmetic and copies ran while one was open for 8% -> 0% of each run, Pallas kernels for 0% -> 0%
where the time goes in v2:
time: 167 us
  Pallas kernels  157 us (94%)
  local copies, waits for them, and re-layouts  7.06 us (4%)
    pallas_call x1, Pallas kernels, blocks_and_gradients(): pl.pallas_call(blocks_kernel, out_shape=(jax.ShapeDtypeStruct((6, 24, 96)...  95.4 us
    pallas_call x1, Pallas kernels, project_and_exchange(): pl.pallas_call(project_kernel, out_shape=jax.ShapeDtypeStruct(blocks, jnp...  61.9 us
    unnamed x4, local copies, waits for them, and re-layouts  6.39 us

profile of v2, /device:TPU:1, one launch (start us, length us, event | category | flops | bytes accessed | tf_op | source)
XLA Modules:
  0.0 166.7 jit_solution(17597209761429819746)
XLA Ops:
  1.3 0.9 multiply_reduce_fusion
  2.2 0.1 iota_add_fusion
  2.3 0.7 add.31.lane_position
  2.9 61.9 %project.1.landed = bf16[32,16,768]{2,1,0:T(8,128)(2,1)} custom-call(bf16[512,8192]{1,0:T(8,128)(2,1)} %bitcast.4, bf16[2048,768]{1,0:T(8,128)(2,1)} %weights.1), custom_call_target="tpu_custom_call" | custom-call | tf_op jit(solution)/shard_map/project/pallas_call | solution.py:176
  64.9 95.4 %blocks.1 = (f32[6,24,96]{2,1,0:T(8,128)}, f32[2,12,192]{2,1,0:T(8,128)}, f32[24,512]{1,0:T(8,128)}, f32[256,768]{1,0:T(8,128)}) custom-call(bf16[32,16,768]{2,1,0:T(8,128)(2,1)} %project.1.landed, s32[1,512]{1,0:T(1,128)} %add.31.lane_position, s32[1]{0:T(128)S(6)} %copy.17.length_ref, s32[128,2048]{1,0:T(8,128)} %bitcast.5, ...), custom_call_target="tpu_custom_call" | custom-call | tf_op jit(solution)/shard_map/blocks/pallas_call | solution.py:634
  160.3 1.4 copy.13
  161.7 1.5 copy.18
  163.2 1.4 copy.19
  164.6 2.1 %copy.20 = f32[1,256,768]{2,1,0:T(8,128)} copy(f32[1,256,768]{2,1,0:T(8,128)} %bitcast.6) | data formatting | bytes 1572864
